TPU v7x, 32 devices: a whole 2x2x4 slice. The times are simulated.
32 devices in a mesh: fsdp: 4 (over z), ctx: 4 (over y, x), tp: 2 (over core).
Axes of the slice: x: 2, y: 2, z: 4, core: 2. Of those that a mesh axis runs over, the one named last changes fastest.
Arguments:
- tokens: bfloat16 [4096, 1024], P(('fsdp', 'ctx')), may hold values from -6 to 6
- lengths: int32 [4, 4], P('fsdp'), may hold values from 1 to 959, as said below
- norm_gain: bfloat16 [1024], P('fsdp'), may hold values from 0.5 to 1.5
- qkv_weight: bfloat16 [3, 1024, 1024], P(None, 'fsdp', 'tp'), may hold values from -0.1875 to 0.1875
- beta_weight: bfloat16 [1024, 8], P('fsdp', 'tp'), may hold values from -0.1875 to 0.1875
- conv_weight: bfloat16 [3, 4, 8, 128], P(None, None, 'tp', 'fsdp'), may hold values from -3 to 3
- head_gain: bfloat16 [128], P('fsdp'), may hold values from 0.5 to 1.5
- out_weight: bfloat16 [1024, 1024], P('tp', 'fsdp'), may hold values from -0.1875 to 0.1875
- mlp_gain: bfloat16 [1024], P('fsdp'), may hold values from 0.5 to 1.5
- gate_up_weight: bfloat16 [2, 1024, 2816], P(None, 'fsdp', 'tp'), may hold values from -0.1875 to 0.1875
- down_weight: bfloat16 [2816, 1024], P('tp', 'fsdp'), may hold values from -0.15625 to 0.15625
- cotangent: bfloat16 [4096, 1024], P(('fsdp', 'ctx')), may hold values from -6 to 6
Outputs:
- layer_out: bfloat16 [4096, 1024], P(('fsdp', 'ctx'))
- input_grad: float32 [4096, 1024], P(('fsdp', 'ctx'))
- norm_gain_grad: float32 [1024], P('fsdp')
- qkv_grad: float32 [3, 1024, 1024], P(None, 'fsdp', 'tp')
- beta_grad: float32 [1024, 8], P('fsdp', 'tp')
- conv_grad: float32 [3, 4, 8, 128], P(None, None, 'tp', 'fsdp')
- head_gain_grad: float32 [128], P('fsdp')
- out_grad: float32 [1024, 1024], P('tp', 'fsdp')
- mlp_gain_grad: float32 [1024], P('fsdp')
- gate_up_grad: float32 [2, 1024, 2816], P(None, 'fsdp', 'tp')
- down_grad: float32 [2816, 1024], P('tp', 'fsdp')
- rms: float32 [5], replicated
Inputs may be any that keep to these rules, and one draw needn't show every extreme that they name: Row g lists the 4 sequence lengths of stream g in order; they sum to at most 1024, the remaining slots at the end are padding. The second sequence of each stream ends at slot 960, so it includes a slot of the first and of the last of its 4 blocks of 256 slots.
All inputs are finite; a program needn't handle non-finite values.
Results may differ from a plain program's by a relative error of at most 0.012.
The roundings to bfloat16 on the way count: a program that leaves them out, or rounds other values in their place, can miss the bound.
Values may be sent and summed in bfloat16 or wider, within the bound.
No kernel may reach another device: no remote copies, remote signals or barrier semaphores. Data moves between devices by JAX's collectives and lax.ppermute only.
A program may use at most 128 MiB of HBM per device.

v0:
```python
import jax
import jax.numpy as jnp
from jax import lax
from jax.sharding import PartitionSpec as P

D = 1024
HD = 128
C = 64
CONV = 4


PRECISE = lax.Precision.HIGHEST
NORM_EPS = 1e-06


def passed_along(value, axis, steps):
    count = lax.axis_size(axis)
    leading, last = (max(0, -steps), min(count, count - steps))
    return lax.ppermute(value, axis, [(source, source + steps) for source in range(leading, last)])


def product(form, left, right):
    return jnp.einsum(form, left, right, precision=PRECISE)


def rounded(values):
    return lax.optimization_barrier(values.astype(jnp.bfloat16)).astype(jnp.float32)


def rms_norm(values, gain):
    return values * lax.rsqrt(jnp.mean(values * values, -1, keepdims=True) + NORM_EPS) * gain


def norm_back(values, gain, grad):
    ratio = lax.rsqrt(jnp.mean(values * values, -1, keepdims=True) + NORM_EPS)
    scaled = values * ratio
    weighted = grad * gain
    value_grad = ratio * (weighted - scaled * jnp.mean(weighted * scaled, -1, keepdims=True))
    gain_grad = jnp.sum((grad * scaled).reshape(-1, values.shape[-1]), 0)
    return (value_grad, gain_grad)


def l2_norm(values):
    return values * lax.rsqrt(jnp.sum(values * values, -1, keepdims=True) + NORM_EPS)


def seq_layout(lengths_row, first, row_count):
    ends = jnp.cumsum(lengths_row)
    places = first + jnp.arange(row_count, dtype=jnp.int32)
    passed = ends[None, :] <= places[:, None]
    begins = jnp.max(jnp.where(passed, ends[None, :], 0), -1)
    seg_ids = jnp.sum(passed.astype(jnp.int32), -1)
    valid = (places < ends[-1]).astype(jnp.float32)
    resets = places == begins
    offsets = places[:, None] - (CONV - 1) + jnp.arange(CONV, dtype=jnp.int32)[None, :]
    taps = (offsets >= begins[:, None]).astype(jnp.float32)
    return (seg_ids, resets, valid, taps)


def block_masks(seg_ids, resets):
    seg_blocks = seg_ids.reshape(-1, C)
    same_seq = (seg_blocks[:, :, None] == seg_blocks[:, None, :]).astype(jnp.float32)
    reset_count = jnp.cumsum(resets.reshape(-1, C).astype(jnp.int32), -1)
    carried = (reset_count == 0).astype(jnp.float32)
    return (same_seq, carried)


def conv_heads(extended, conv_taps, taps):
    row_count = taps.shape[0]
    total = jnp.zeros((row_count,) + extended.shape[1:], jnp.float32)
    for offset in range(CONV):
        total = (
            total
            + extended[offset : offset + row_count]
            * conv_taps[:, offset][None]
            * taps[:, offset][:, None, None]
        )
    activated = jax.nn.silu(total)
    head_count = extended.shape[2] // HD
    split_rows = activated.reshape(row_count, 3, head_count, HD)
    return (l2_norm(split_rows[:, 0]), l2_norm(split_rows[:, 1]), split_rows[:, 2])


def to_blocks(values):
    return values.reshape(values.shape[0] // C, C, values.shape[1], values.shape[2]).transpose(
        2, 0, 1, 3
    )


def beta_blocks(values):
    return values.reshape(values.shape[0] // C, C, values.shape[1]).transpose(2, 0, 1)


def from_blocks(values):
    return values.transpose(1, 2, 0, 3).reshape(-1, values.shape[0], values.shape[3])


def unit_inverse(lower):
    size_now = lower.shape[-1]
    identity = jnp.eye(size_now, dtype=jnp.float32)
    inverse = identity - lower
    power = lower
    span = 2
    while span < size_now:
        power = product("...ij,...jk->...ik", power, power)
        inverse = product("...ij,...jk->...ik", inverse, identity + power)
        span = span * 2
    return inverse


def block_terms(queries, key_rows, value_rows, beta_rows, same_seq, carried):
    wide = key_rows.shape[-1]
    last_seg = same_seq[:, -1, :]
    key_gram = product("hncd,hnmd->hncm", key_rows, key_rows)
    lower = jnp.tril(beta_rows[..., :, None] * key_gram * same_seq, -1)
    inverse = unit_inverse(lower)
    stacked = beta_rows[..., None] * jnp.concatenate([key_rows, value_rows], -1)
    solved = product("hncm,hnmd->hncd", inverse, stacked)
    w_part = solved[..., :wide]
    u_part = solved[..., wide:]
    query_key = jnp.tril(product("hncd,hnmd->hncm", queries, key_rows) * same_seq)
    keep_all = carried[:, -1]
    trans = keep_all[:, None, None] * jnp.eye(wide, dtype=jnp.float32) - product(
        "hnci,hncj->hnij", w_part * (carried * last_seg)[..., None], key_rows
    )
    push = product("hnci,hncj->hnij", u_part * last_seg[..., None], key_rows)
    return (w_part, u_part, query_key, queries, trans, push)


def run_blocks(terms, carried, start_state):
    sequenced = tuple((jnp.moveaxis(piece, 1, 0) for piece in terms)) + (carried,)

    def advance(state, pieces):
        w_now, u_now, qk_now, q_now, trans_now, push_now, carry_now = pieces
        carry_col = carry_now[None, :, None]
        from_state = product("hcd,hvd->hcv", w_now, state)
        fresh = u_now - carry_col * from_state
        output = carry_col * product("hcd,hvd->hcv", q_now, state) + product(
            "hcm,hmv->hcv", qk_now, fresh
        )
        following = product("hvk,hkj->hvj", state, trans_now) + push_now
        return (following, output)

    final_state, outputs = lax.scan(advance, start_state, sequenced)
    return (jnp.moveaxis(outputs, 0, 1), final_state)


def join_maps(earlier, later):
    return (
        product("hik,hkj->hij", earlier[0], later[0]),
        product("hvk,hkj->hvj", earlier[1], later[0]) + later[1],
    )


def row_total(values, valid):
    return jnp.sum(valid * jnp.sum(values * values, -1))


def local(
    tokens,
    lengths,
    norm_gain,
    qkv_weight,
    beta_weight,
    conv_weight,
    head_gain,
    out_weight,
    mlp_gain,
    gate_up_weight,
    down_weight,
    cotangent,
):
    row_count = tokens.shape[0]
    ctx_count = lax.axis_size("ctx")
    fsdp_count = lax.axis_size("fsdp")
    seg_ids, resets, valid, taps = seq_layout(
        lengths[0], lax.axis_index("ctx") * row_count, row_count
    )
    same_seq, carried = block_masks(seg_ids, resets)
    gathered = (
        lax.all_gather(norm_gain, "fsdp", axis=0, tiled=True),
        lax.all_gather(qkv_weight, "fsdp", axis=1, tiled=True),
        lax.all_gather(beta_weight, "fsdp", axis=0, tiled=True),
        lax.all_gather(conv_weight, "fsdp", axis=3, tiled=True),
        lax.all_gather(head_gain, "fsdp", axis=0, tiled=True),
        lax.all_gather(out_weight, "fsdp", axis=1, tiled=True),
        lax.all_gather(mlp_gain, "fsdp", axis=0, tiled=True),
        lax.all_gather(gate_up_weight, "fsdp", axis=1, tiled=True),
        lax.all_gather(down_weight, "fsdp", axis=1, tiled=True),
    )
    (
        first_gain,
        qkv_full,
        beta_full,
        conv_full,
        head_full,
        out_full,
        second_gain,
        gate_up_full,
        down_full,
    ) = gathered
    heads_local = beta_full.shape[1]
    width_local = qkv_full.shape[2]
    x_wide = tokens.astype(jnp.float32)
    first_f = first_gain.astype(jnp.float32)
    second_f = second_gain.astype(jnp.float32)
    head_f = head_full.astype(jnp.float32)
    normed_in = rms_norm(x_wide, first_f).astype(jnp.bfloat16)
    projected = jnp.einsum(
        "td,idk->tik", normed_in, qkv_full, preferred_element_type=jnp.float32
    ).astype(jnp.bfloat16)
    beta_rows = jax.nn.sigmoid(jnp.dot(normed_in, beta_full, preferred_element_type=jnp.float32))
    rim_rows = passed_along(projected[row_count - (CONV - 1) :], "ctx", 1)
    extended = jnp.concatenate([rim_rows, projected], 0).astype(jnp.float32)
    conv_local = conv_full.reshape(3, CONV, width_local).astype(jnp.float32)

    def conv_part(ext_rows, conv_taps):
        return conv_heads(ext_rows, conv_taps, taps)

    (query_raw, key_raw, value_raw), conv_pull = jax.vjp(conv_part, extended, conv_local)
    queries = rounded(query_raw)
    key_rows = rounded(key_raw)
    value_rows = rounded(value_raw)

    def prepare(query_in, key_in, value_in, beta_in):
        return block_terms(
            to_blocks(query_in) * HD ** (-0.5),
            to_blocks(key_in),
            to_blocks(value_in),
            beta_blocks(beta_in),
            same_seq,
            carried,
        )

    terms, prepare_pull = jax.vjp(prepare, queries, key_rows, value_rows, beta_rows)
    identity = jnp.broadcast_to(jnp.eye(HD, dtype=jnp.float32), (heads_local, HD, HD))
    empty_state = jnp.zeros((heads_local, HD, HD), jnp.float32)

    def compose(accum, pieces):
        return (join_maps(accum, pieces), None)

    (device_map, device_shift), ignored = lax.scan(
        compose,
        (identity, empty_state),
        (jnp.moveaxis(terms[4], 1, 0), jnp.moveaxis(terms[5], 1, 0)),
    )
    incoming = empty_state
    for repeat in range(ctx_count - 1):
        incoming = passed_along(
            product("hvk,hkj->hvj", incoming, device_map) + device_shift, "ctx", 1
        )

    def run_part(term_in, state_in):
        return run_blocks(term_in, carried, state_in)

    (out_blocks, ignored_state), run_pull = jax.vjp(run_part, terms, incoming)
    mixed_out = from_blocks(out_blocks)
    head_normed = rms_norm(mixed_out, head_f).reshape(row_count, width_local).astype(jnp.bfloat16)
    attn_rows = (
        lax.psum(jnp.dot(head_normed, out_full, preferred_element_type=jnp.float32), "tp")
        * valid[:, None]
    )
    middle = x_wide + attn_rows
    normed_mid = rms_norm(middle, second_f).astype(jnp.bfloat16)
    gate_up = jnp.einsum(
        "td,idf->tif", normed_mid, gate_up_full, preferred_element_type=jnp.float32
    )
    gate_rows = gate_up[:, 0]
    up_rows = gate_up[:, 1]
    activated = (jax.nn.silu(gate_rows) * up_rows).astype(jnp.bfloat16)
    ffn_rows = (
        lax.psum(jnp.dot(activated, down_full, preferred_element_type=jnp.float32), "tp")
        * valid[:, None]
    )
    result = middle + ffn_rows
    stat_sums = jnp.stack(
        [
            row_total(x_wide, valid),
            row_total(attn_rows, valid),
            row_total(middle, valid),
            row_total(ffn_rows, valid),
            row_total(result, valid),
            jnp.sum(valid),
        ]
    )
    out_cot = cotangent.astype(jnp.float32)
    ffn_back = (out_cot * valid[:, None]).astype(jnp.bfloat16)
    down_grad = jnp.einsum("tf,td->fd", activated, ffn_back, preferred_element_type=jnp.float32)
    act_grad = jnp.einsum("td,fd->tf", ffn_back, down_full, preferred_element_type=jnp.float32)
    gate_sig = jax.nn.sigmoid(gate_rows)
    up_grad = act_grad * gate_rows * gate_sig
    gate_grad = act_grad * up_rows * gate_sig * (1.0 + gate_rows * (1.0 - gate_sig))
    gate_up_back = jnp.stack([gate_grad, up_grad], 1).astype(jnp.bfloat16)
    gate_up_grad = jnp.einsum(
        "td,tif->idf", normed_mid, gate_up_back, preferred_element_type=jnp.float32
    )
    mid_part = jnp.einsum(
        "tif,idf->td", gate_up_back, gate_up_full, preferred_element_type=jnp.float32
    )
    mid_grad = lax.psum(mid_part, "tp")
    middle_norm_grad, second_gain_grad = norm_back(middle, second_f, mid_grad)
    middle_grad = out_cot + middle_norm_grad
    attn_back = (middle_grad * valid[:, None]).astype(jnp.bfloat16)
    out_grad = jnp.einsum("tk,td->kd", head_normed, attn_back, preferred_element_type=jnp.float32)
    head_in_grad = jnp.einsum(
        "td,kd->tk", attn_back, out_full, preferred_element_type=jnp.float32
    ).reshape(row_count, heads_local, HD)
    mixed_grad, head_gain_part = norm_back(mixed_out, head_f, head_in_grad)
    mixed_blocks = to_blocks(mixed_grad)

    def state_part(state_in):
        return run_blocks(terms, carried, state_in)[0]

    ignored_out, state_pull = jax.vjp(state_part, incoming)
    local_state = state_pull(mixed_blocks)[0]
    map_turned = jnp.swapaxes(device_map, 1, 2)
    outgoing = empty_state
    for repeat in range(ctx_count - 1):
        outgoing = passed_along(
            local_state + product("hvk,hkj->hvj", outgoing, map_turned), "ctx", -1
        )
    term_grads, ignored_grad = run_pull((mixed_blocks, outgoing))
    query_grad, key_grad, value_grad, beta_row_grad = prepare_pull(term_grads)
    logit_grad = (beta_row_grad * beta_rows * (1.0 - beta_rows)).astype(jnp.bfloat16)
    ext_grad, conv_grad_flat = conv_pull((query_grad, key_grad, value_grad))
    back_rim = passed_along(ext_grad[: CONV - 1], "ctx", -1)
    proj_grad = ext_grad[CONV - 1 :] + jnp.concatenate(
        [jnp.zeros((row_count - (CONV - 1),) + back_rim.shape[1:], jnp.float32), back_rim], 0
    )
    proj_back = proj_grad.astype(jnp.bfloat16)
    qkv_grad = jnp.einsum("td,tik->idk", normed_in, proj_back, preferred_element_type=jnp.float32)
    beta_grad = jnp.einsum("td,th->dh", normed_in, logit_grad, preferred_element_type=jnp.float32)
    in_part = jnp.einsum(
        "tik,idk->td", proj_back, qkv_full, preferred_element_type=jnp.float32
    ) + jnp.einsum("th,dh->td", logit_grad, beta_full, preferred_element_type=jnp.float32)
    in_grad, head_gain_grad = lax.psum((in_part, head_gain_part), "tp")
    x_norm_grad, first_gain_grad = norm_back(x_wide, first_f, in_grad)
    input_grad = middle_grad + x_norm_grad
    stat_rows = jnp.broadcast_to(stat_sums[None, :], (fsdp_count, stat_sums.shape[0]))
    conv_grad = conv_grad_flat.reshape(3, CONV, heads_local, HD)
    shares = (
        lax.psum_scatter(first_gain_grad, "fsdp", scatter_dimension=0, tiled=True),
        lax.psum_scatter(qkv_grad, "fsdp", scatter_dimension=1, tiled=True),
        lax.psum_scatter(beta_grad, "fsdp", scatter_dimension=0, tiled=True),
        lax.psum_scatter(conv_grad, "fsdp", scatter_dimension=3, tiled=True),
        lax.psum_scatter(head_gain_grad, "fsdp", scatter_dimension=0, tiled=True),
        lax.psum_scatter(out_grad, "fsdp", scatter_dimension=1, tiled=True),
        lax.psum_scatter(second_gain_grad, "fsdp", scatter_dimension=0, tiled=True),
        lax.psum_scatter(gate_up_grad, "fsdp", scatter_dimension=1, tiled=True),
        lax.psum_scatter(down_grad, "fsdp", scatter_dimension=1, tiled=True),
        lax.psum_scatter(stat_rows, "fsdp", scatter_dimension=0, tiled=True),
    )
    totals = lax.psum(
        (
            shares[0],
            shares[1],
            shares[2],
            shares[3],
            shares[4],
            shares[5],
            shares[6],
            shares[7],
            shares[8],
            shares[9],
        ),
        "ctx",
    )
    stat_total = totals[9][0]
    rms = jnp.sqrt(stat_total[:5] / (stat_total[5] * D))
    return (
        result.astype(jnp.bfloat16),
        input_grad,
        totals[0],
        totals[1],
        totals[2],
        totals[3],
        totals[4],
        totals[5],
        totals[6],
        totals[7],
        totals[8],
        rms,
    )


def solution(mesh):
    return jax.shard_map(
        local,
        mesh=mesh,
        in_specs=(
            P(("fsdp", "ctx"), None),
            P("fsdp", None),
            P("fsdp"),
            P(None, "fsdp", "tp"),
            P("fsdp", "tp"),
            P(None, None, "tp", "fsdp"),
            P("fsdp"),
            P("tp", "fsdp"),
            P("fsdp"),
            P(None, "fsdp", "tp"),
            P("tp", "fsdp"),
            P(("fsdp", "ctx"), None),
        ),
        out_specs=(
            P(("fsdp", "ctx"), None),
            P(("fsdp", "ctx"), None),
            P("fsdp"),
            P(None, "fsdp", "tp"),
            P("fsdp", "tp"),
            P(None, None, "tp", "fsdp"),
            P("fsdp"),
            P("tp", "fsdp"),
            P("fsdp"),
            P(None, "fsdp", "tp"),
            P("tp", "fsdp"),
            P(),
        ),
        check_vma=False,
    )
```

profile of v0, /device:TPU:0, one launch (start us, length us, event | category | flops | bytes accessed | tf_op | source)
XLA Modules:
  0.0 1154.2 jit_solution(13363397626016956386)
XLA Ops:
  10.7 12.6 %all-gather = bf16[4,1,256]{2,1,0:T(2,128)(2,1)S(1)} all-gather(bf16[1,1,256]{2,1,0:T(2,128)(2,1)S(1)} %reshape.331), channel_id=1, replica_groups=mesh['fsdp'=4,'ctx'=4,'tp'=2] {'fsdp'}, dimensions={0}, use_global_device_ids=true | all-gather | bytes 2560 | tf_op jit(solution)/shard_map/all_gather | solution.py:181
  24.0 17.8 %all_gather.30 = bf16[3,4,4,128]{2,1,0,3:T(4,128)(2,1)S(1)} all-gather(bf16[3,4,4,32]{2,1,0,3:T(4,128)(2,1)S(1)} %copy.589), channel_id=1, replica_groups=mesh['fsdp'=4,'ctx'=4,'tp'=2] {'fsdp'}, dimensions={3}, use_global_device_ids=true | all-gather | bytes 15360 | tf_op jit(solution)/shard_map/all_gather | solution.py:184
  42.4 12.2 %all_gather.28 = bf16[1024,4]{0,1:T(4,128)(2,1)S(1)} all-gather(bf16[256,4]{0,1:T(4,128)(2,1)S(1)} %copy-done.132), channel_id=1, replica_groups=mesh['fsdp'=4,'ctx'=4,'tp'=2] {'fsdp'}, dimensions={0}, use_global_device_ids=true | all-gather | bytes 10240 | tf_op jit(solution)/shard_map/all_gather | solution.py:183
  57.8 11.3 all-reduce.14
  70.2 11.6 %all-gather.7.cloned.1.call-done = bf16[3,1024,512]{2,1,0:T(8,128)(2,1)} async-done(((bf16[3,256,512]{2,1,0:T(8,128)(2,1)}), bf16[3,1024,512]{2,1,0:T(8,128)(2,1)}) %all-gather.7.cloned.1.call-update) | async-done | bytes 3145744 | tf_op jit(solution)/shard_map/all_gather | solution.py:182
  127.2 13.8 %while.85 = (s32[]{:T(128)}, f32[4,128,128]{1,2,0:T(8,128)S(1)}, f32[4,128,128]{1,2,0:T(8,128)}, f32[4,4,128,128]{2,3,1,0:T(8,128)S(1)}, f32[4,4,128,128]{2,3,1,0:T(8,128)}, /*index=5*/s32[]{:T(128)}, s32[]{:T(128)}) while((s32[]{:T(128)}, f32[4,128,128]{1,2,0:T(8,128)S(1)}, f32[4,128,128]{1,2,0:T(8,128)}, ...), condition=%wide.region_7.8_spmd.clone, body=%wide.region_6.7_spmd.clone.sunk | while | flops 201457664 | bytes 2884699 | solution.py:242
  144.7 4.2 collective-permute-start.1
  154.0 4.4 collective-permute-start.2
  162.9 5.9 collective-permute-start.3
  173.9 33.4 %while.82 = (s32[]{:T(128)}, f32[4,128,128]{1,2,0:T(8,128)}, f32[4,4,64,128]{3,2,1,0:T(8,128)}, f32[4,4,128,128]{2,3,1,0:T(8,128)S(1)}, f32[4,1,64,1]{2,3,1,0:T(...) while((s32[]{:T(128)}, f32[4,128,128]{1,2,0:T(8,128)}, ...), condition=%wide.region_10.11_spmd, body=%wide.region_9.10_spmd.sunk | while | flops 226689024 | bytes 3937937 | solution.py:144
  216.9 9.6 all-gather.1
  227.7 9.6 all-reduce.28.cloned.1.call-done
  239.1 107.7 %all-gather.11.cloned.1.call-done = bf16[2,1024,1408]{2,1,0:T(8,128)(2,1)} async-done(((bf16[2,256,1408]{2,1,0:T(8,128)(2,1)}), bf16[2,1024,1408]{2,1,0:T(8,128)(2,1)}) %all-gather.11.cloned.1.call-update) | async-done | bytes 5767184 | tf_op jit(solution)/shard_map/all_gather | solution.py:188
  346.8 5.9 fusion.207
  352.7 53.0 %all-gather.13.cloned.1.call-done = bf16[1408,1024]{1,0:T(8,128)(2,1)} async-done(((bf16[1408,256]{1,0:T(8,128)(2,1)}), bf16[1408,1024]{1,0:T(8,128)(2,1)}) %all-gather.13.cloned.1.call-update) | async-done | bytes 2883600 | tf_op jit(solution)/shard_map/all_gather | solution.py:189
  405.7 4.4 fusion.133
  421.6 12.9 %all-reduce.34.cloned.1.call-done = (f32[256,1024]{1,0:T(8,128)}, f32[256,1024]{1,0:T(8,128)}) async-done(((f32[256,1024]{1,0:T(8,128)}, f32[256,1024]{1,0:T(8,128)}), (f32[256,1024]{1,0:T(8,128)}, f32[256,1024]{1,0:T(8,128)})) %all-reduce.34.cloned.1.call-update) | async-done | bytes 2097168 | tf_op jit(solution)/shard_map/psum | solution.py:272
  448.6 22.0 %while.86 = (s32[]{:T(128)}, f32[4,128,128]{1,2,0:T(8,128)}, f32[4,4,128,128]{3,2,1,0:T(8,128)}, f32[4,1,64,1]{2,3,1,0:T(1,128)S(1)}, f32[4,4,64,128]{3,2,1,0:T(...) while((s32[]{:T(128)}, f32[4,128,128]{1,2,0:T(8,128)}, ...), condition=%wide.region_21.22_spmd.clone, body=%wide.region_20.21_spmd.clone.sunk | while | flops 226787328 | bytes 2756239 | solution.py:144
  475.1 9.1 collective-permute-done.4
  486.8 9.3 collective-permute-done.5
  502.1 5.2 collective-permute-done.6
  513.9 51.4 %while.84 = (s32[]{:T(128)}, f32[4,128,128]{1,2,0:T(8,128)S(1)}, f32[4,4,64,128]{3,2,0,1:T(8,128)}, f32[4,4,64,128]{3,2,0,1:T(8,128)}, f32[4,4,64,64]{2,3,1,0:T(...) while((s32[]{:T(128)}, f32[4,128,128]{1,2,0:T(8,128)S(1)}, ...), condition=%wide.region_23.24_spmd, body=%wide.region_22.23_spmd.sunk | while | flops 453312512 | bytes 9840861 | solution.py:144
  606.9 4.2 collective-permute-done.7
  616.1 8.1 convolution_bitcast_fusion.9
  633.7 93.4 %reduce-scatter.11.cloned.1.call-done = f32[3,256,512]{1,2,0:T(8,128)} async-done(((f32[3,1024,512]{1,2,0:T(8,128)}), f32[3,256,512]{1,2,0:T(8,128)}) %reduce-scatter.11.cloned.1.call-update) | async-done | bytes 1572880 | tf_op jit(solution)/shard_map/reduce_scatter | solution.py:343
  727.1 197.8 %reduce-scatter.15.cloned.1.call-done = f32[2,256,1408]{1,2,0:T(8,128)} async-done(((f32[2,1024,1408]{1,2,0:T(8,128)}), f32[2,256,1408]{1,2,0:T(8,128)}) %reduce-scatter.15.cloned.1.call-update) | async-done | bytes 2883600 | tf_op jit(solution)/shard_map/reduce_scatter | solution.py:349
  931.4 19.1 %reduce-scatter.19.cloned.1.call-done = f32[256,4]{1,0:T(8,128)} async-done(((f32[1024,4]{1,0:T(8,128)}), f32[256,4]{1,0:T(8,128)}) %reduce-scatter.19.cloned.1.call-update) | async-done | bytes 4112
  951.5 19.1 %reduce-scatter.21.cloned.1.call-done = f32[32,48]{1,0:T(8,128)} async-done(((f32[128,48]{1,0:T(8,128)}), f32[32,48]{1,0:T(8,128)}) %reduce-scatter.21.cloned.1.call-update) | async-done | bytes 6160
  971.6 19.7 %all-reduce.30.cloned.1.call-done = f32[256,1024]{1,0:T(8,128)} async-done(((f32[256,1024]{1,0:T(8,128)}), f32[256,1024]{1,0:T(8,128)}) %all-reduce.30.cloned.1.call-update) | async-done | bytes 1048592 | tf_op jit(solution)/shard_map/psum | solution.py:336
  993.1 19.0 %all-reduce.21 = (f32[1024]{0:T(1024)S(1)}, f32[128]{0:T(128)S(1)}, f32[1024]{0:T(1024)S(1)}, f32[4,6]{1,0:T(4,128)S(1)}) all-reduce(f32[1024]{0:T(1024)S(1)} %get-tuple-element.993, f32[128]{0:T(128)S(1)} %multiply_reduce_fusion.10, f32[1024]{0:T(1024)S(1)} %copy-done.116, ...), channel_id=2, replica_groups=mesh['fsdp'=4,'ctx'=4,'tp'=2] {'fsdp'}, use_global_device_ids=true, to_apply=%region_31.32.clone | all-reduce | flops 2200 | bytes 17600
  1015.3 17.8 %all-reduce.19 = (f32[256]{0:T(256)}, f32[256,4]{0,1:T(4,128)}, f32[3,4,4,32]{3,2,1,0:T(4,128)}, f32[32]{0:T(128)}, f32[256]{0:T(256)}, /*index=5*/f32[1,6]{1,0:T(1,128)S(1)}) all-reduce(f32[256]{0:T(256)S(1)} %dynamic-slice.2, f32[256,4]{0,1:T(4,128)S(1)} %copy.747, ...), channel_id=1, replica_groups=mesh['fsdp'=4,'ctx'=4,'tp'=2] {'ctx'}, use_global_device_ids=true, to_apply=%region_32.33 | all-reduce | flops 3110 | bytes 24880 | tf_op jit(solution)/shard_map/psum | solution.py:353
  1036.2 103.1 %all-reduce.32.cloned.1.call-done = (f32[3,256,512]{1,2,0:T(8,128)}, f32[512,256]{1,0:T(8,128)}, f32[2,256,1408]{1,2,0:T(8,128)}, f32[1408,256]{1,0:T(8,128)}) async-done(((f32[3,256,512]{1,2,0:T(8,128)}, f32[512,256]{1,0:T(8,128)}, f32[2,256,1408]{1,2,0:T(8,128)}, f32[1408,256]{1,0:T(8,128)}), (f32[3,256,512]{1,2,0:T(8,128)}, f32[512,256]{1,0:T(8,128)}, f32[2,256,1408]{1,2,0:T(8,128)}, ...) | async-done | bytes 6422544 | tf_op jit(solution)/shard_map/psum | solution.py:353
  (662 shorter events, 329.1 us)
Async XLA Ops:
  7.2 62.6 %copy-start.11 = (bf16[256,1024]{1,0:T(8,128)(2,1)S(1)}, bf16[256,1024]{1,0:T(8,128)(2,1)}, u32[]{:S(2)}) copy-start(bf16[256,1024]{1,0:T(8,128)(2,1)} %param.22) | copy-start | bytes 1572868
  7.3 74.5 %all-gather.7.cloned.1.call-start = ((), (), s32[]{:S(2)}) async-start(), calls=%async_computation.6 | async-start | bytes 3932160 | tf_op jit(solution)/shard_map/all_gather | solution.py:182
  8.0 204.4 %all-gather.9.cloned.1.call-start = ((), (), s32[]{:S(2)}) async-start(), calls=%async_computation.7 | async-start | bytes 1310720 | tf_op jit(solution)/shard_map/all_gather | solution.py:186
  8.7 228.6 %all-reduce.28.cloned.1.call-start = ((), (), s32[]{:S(2)}) async-start(), calls=%async_computation.8 | async-start | bytes 2097152 | tf_op jit(solution)/shard_map/psum | solution.py:260
  10.7 74.1 %copy-start.106 = (f32[256]{0:T(256)}, f32[256]{0:T(256)S(1)}, u32[]{:S(2)}) copy-start(f32[256]{0:T(256)S(1)} %add_rsqrt_fusion.4) | copy-start | bytes 3076
  23.7 66.1 %copy-start.108 = (f32[256,1]{0,1:T(1,128)}, f32[256,1]{0,1:T(1,128)S(1)}, u32[]{:S(2)}) copy-start(f32[256,1]{0,1:T(1,128)S(1)} %get-tuple-element.1145) | copy-start | bytes 3076
  23.7 66.1 %copy-start.110 = (f32[256,1]{0,1:T(1,128)}, f32[256,1]{0,1:T(1,128)S(1)}, u32[]{:S(2)}) copy-start(f32[256,1]{0,1:T(1,128)S(1)} %get-tuple-element.1146) | copy-start | bytes 3076
  23.7 66.1 %copy-start.112 = (f32[256,1]{0,1:T(1,128)}, f32[256,1]{0,1:T(1,128)S(1)}, u32[]{:S(2)}) copy-start(f32[256,1]{0,1:T(1,128)S(1)} %get-tuple-element.1147) | copy-start | bytes 3076
  23.7 66.1 %copy-start.114 = (f32[256,1]{0,1:T(1,128)}, f32[256,1]{0,1:T(1,128)S(1)}, u32[]{:S(2)}) copy-start(f32[256,1]{0,1:T(1,128)S(1)} %get-tuple-element.1148) | copy-start | bytes 3076
  84.8 4.8 collective-permute-start
  144.7 8.6 collective-permute-start.1
  154.0 8.3 collective-permute-start.2
  162.9 9.0 collective-permute-start.3
  215.1 131.6 %all-gather.11.cloned.1.call-start = ((), (), s32[]{:S(2)}) async-start(), calls=%async_computation.9 | async-start | bytes 7208960 | tf_op jit(solution)/shard_map/all_gather | solution.py:188
  215.7 190.0 %all-gather.13.cloned.1.call-start = ((), (), s32[]{:S(2)}) async-start(), calls=%async_computation.10 | async-start | bytes 3604480 | tf_op jit(solution)/shard_map/all_gather | solution.py:189
  216.3 218.2 %all-reduce.34.cloned.1.call-start = ((), (), s32[]{:S(2)}) async-start(), calls=%async_computation.19 | async-start | bytes 4194304 | tf_op jit(solution)/shard_map/psum | solution.py:272
  239.0 113.7 %copy-start.122 = (f32[256]{0:T(256)}, f32[256]{0:T(256)S(1)}, u32[]{:S(2)}) copy-start(f32[256]{0:T(256)S(1)} %get-tuple-element.1115) | copy-start | bytes 3076
  239.0 199.4 %copy-start = (f32[256,1024]{1,0:T(8,128)}, f32[256,1024]{1,0:T(8,128)S(1)}, u32[]{:S(2)}) copy-start(f32[256,1024]{1,0:T(8,128)S(1)} %get-tuple-element.1116) | copy-start | bytes 3145732
  239.1 199.4 %copy-start.96 = (f32[256]{0:T(256)}, f32[256]{0:T(256)S(1)}, u32[]{:S(2)}) copy-start(f32[256]{0:T(256)S(1)} %add_rsqrt_fusion.3) | copy-start | bytes 3076
  414.9 218.8 %reduce-scatter.13.cloned.1.call-start = ((), (), s32[]{:S(2)}) async-start(), calls=%async_computation.13 | async-start | bytes 2621440 | tf_op jit(solution)/shard_map/reduce_scatter | solution.py:347
  447.6 186.1 %reduce-scatter.17.cloned.1.call-start = ((), (), s32[]{:S(2)}) async-start(), calls=%async_computation.15 | async-start | bytes 7208960 | tf_op jit(solution)/shard_map/reduce_scatter | solution.py:350
  473.8 10.4 collective-permute-start.4
  485.5 10.6 collective-permute-start.5
  497.2 10.0 collective-permute-start.6
  502.0 225.1 %reduce-scatter.11.cloned.1.call-start = ((), (), s32[]{:S(2)}) async-start(), calls=%async_computation.12 | async-start | bytes 7864320 | tf_op jit(solution)/shard_map/reduce_scatter | solution.py:343
  604.7 6.5 collective-permute-start.7
  614.9 309.9 %reduce-scatter.15.cloned.1.call-start = ((), (), s32[]{:S(2)}) async-start(), calls=%async_computation.14 | async-start | bytes 14417920 | tf_op jit(solution)/shard_map/reduce_scatter | solution.py:349
  624.3 326.3 %reduce-scatter.19.cloned.1.call-start = ((), (), s32[]{:S(2)}) async-start(), calls=%async_computation.16 | async-start | bytes 655360
  627.6 343.0 %reduce-scatter.21.cloned.1.call-start = ((), (), s32[]{:S(2)}) async-start(), calls=%async_computation.17 | async-start | bytes 81920
  629.1 362.2 %all-reduce.30.cloned.1.call-start = ((), (), s32[]{:S(2)}) async-start(), calls=%async_computation.11 | async-start | bytes 2097152 | tf_op jit(solution)/shard_map/psum | solution.py:336
  633.6 505.7 %all-reduce.32.cloned.1.call-start = ((), (), s32[]{:S(2)}) async-start(), calls=%async_computation.18 | async-start | bytes 12845056 | tf_op jit(solution)/shard_map/psum | solution.py:353
  931.2 103.7 %copy-start.21 = (f32[256,1024]{1,0:T(8,128)S(1)}, f32[256,1024]{1,0:T(8,128)}, u32[]{:S(2)}) copy-start(f32[256,1024]{1,0:T(8,128)} %copy-done.20) | copy-start | bytes 3145732
  (136 other events, 926.5 us)
Sparse Core Ops, SparseCore 0:
  9.7 72.0 all-gather.6
  83.3 29.4 all-gather.8
  215.2 22.0 all-reduce.27
  238.8 107.8 all-gather.10
  348.3 57.4 all-gather.12
  415.0 19.4 all-reduce.33
  447.7 45.0 reduce-scatter.12
  502.1 105.3 reduce-scatter.16
  615.1 111.9 reduce-scatter.10
  729.4 195.4 reduce-scatter.14
  927.8 22.6 reduce-scatter.18
  953.3 17.2 reduce-scatter.20
  973.5 17.7 all-reduce.29
  995.5 143.7 all-reduce.31
where the time goes:
time: 1160 us; the launch traced here: 1150 us
  waiting for transfers between devices  684 us (59%)
  matrix products  210 us (18%)
  blocking collectives  103 us (9%)
  local copies, waits for them, and re-layouts  84.7 us (7%)
  other arithmetic  28.9 us (2%)
  starting transfers between devices  24 us (2%)
  between operations  19.1 us (2%)
    reduce_scatter x1, waiting for transfers between devices, local(): lax.psum_scatter(gate_up_grad, 'fsdp', scatter_dimension=1, tiled=True)  198 us
    dot_general x123, matrix products, product(): return jnp.einsum(form, left, right, precision=PRECISE)  163 us
    all_gather x1, waiting for transfers between devices, local(): lax.all_gather(gate_up_weight, 'fsdp', axis=1, tiled=True)  108 us
    psum x1, waiting for transfers between devices, local(): lax.psum((shares[0], shares[1], shares[2], shares[3], shares[4], shares[5...  103 us
    reduce_scatter x1, waiting for transfers between devices, local(): lax.psum_scatter(qkv_grad, 'fsdp', scatter_dimension=1, tiled=True)  93.4 us
    all_gather x1, waiting for transfers between devices, local(): lax.all_gather(down_weight, 'fsdp', axis=1, tiled=True)  53 us
    unnamed x16, waiting for transfers between devices  40.8 us
    ppermute x8, waiting for transfers between devices, passed_along(): lax.ppermute(value, axis, [(source, source + steps) for source in range(l...  34.1 us
  transfers between devices with their start and end apart: 22, of which 18 were waited for; matrix products, arithmetic and copies ran while one was open for 25% of the time, Pallas kernels for 0%

commit v1 on v0

v1 whole, which is shorter than its diff:
```python
import functools

import jax
import jax.numpy as jnp
from jax import lax
from jax.experimental import pallas as pl
from jax.experimental.pallas import tpu as pltpu
from jax.sharding import PartitionSpec as P

HD = 128
CONV = 4
PAD = 8
EPS = 1e-06
F32 = jnp.float32
BF16 = jnp.bfloat16
NN = (((1,), (0,)), ((), ()))
NT = (((1,), (1,)), ((), ()))
TN = (((0,), (0,)), ((), ()))
SCALE = HD ** (-0.5)


def parts_of(value, count):
    if value.dtype == BF16:
        return [value]
    pieces = []
    for left in range(count):
        piece = value.astype(BF16)
        pieces.append(piece)
        if left + 1 < count:
            value = value - piece.astype(F32)
    return pieces


def mm(left, right, dims=NN, split=2):
    lefts, rights = parts_of(left, split), parts_of(right, split)
    total = None
    for i, a in enumerate(lefts):
        for j, b in enumerate(rights):
            if i + j < max(len(lefts), len(rights)):
                term = lax.dot_general(a, b, dims, preferred_element_type=F32)
                total = term if total is None else total + term
    return total


def sigmoid(v):
    return 1.0 / (1.0 + jnp.exp(-v))


def unit_lower_inverse(lower):
    n = lower.shape[0]
    row = lax.broadcasted_iota(jnp.int32, (n, n), 0)
    col = lax.broadcasted_iota(jnp.int32, (n, n), 1)
    inverse = jnp.where(row == col, 1.0, 0.0) - jnp.where(row // 2 == col // 2, lower, 0.0)
    size = 2
    while size < n:
        inside = (row // (2 * size) == col // (2 * size)) & (row // size != col // size)
        step = jnp.where(inside, lower, 0.0)
        inverse = inverse - mm(inverse, mm(step, inverse))
        size *= 2
    return inverse


def conv_forward(ext_ref, taps, age, rows):
    total = jnp.zeros((rows, HD), F32)
    for k in range(CONV):
        reach = CONV - 1 - k
        rows_k = ext_ref[pl.ds(PAD - reach, rows), :]
        total = total + jnp.where(age >= reach, rows_k, 0.0) * taps[k : k + 1]
    return total


def l2_ratio(values):
    return lax.rsqrt(jnp.sum(values * values, -1, keepdims=True) + EPS)


def terms_kernel(x_ref, w_ref, taps_ref, beta_ref, lb_ref, pre_ref, qkv_ref, tt_ref, y_ref, ms_ref, ext):
    rows = lb_ref.shape[0]
    lb = lb_ref[...]
    place = lax.broadcasted_iota(jnp.int32, (rows, 1), 0)
    age = place - lb
    row = lax.broadcasted_iota(jnp.int32, (rows, rows), 0)
    col = lax.broadcasted_iota(jnp.int32, (rows, rows), 1)
    same = col >= lb
    lb_last = lb_ref[pl.ds(rows - 1, 1), :]
    last = jnp.where(place >= lb_last, 1.0, 0.0)
    keep = jnp.where(lb_last < 0, 1.0, 0.0)
    eye = jnp.where(lax.broadcasted_iota(jnp.int32, (HD, HD), 0) == lax.broadcasted_iota(jnp.int32, (HD, HD), 1), 1.0, 0.0)
    out = []
    for i in range(3):
        pre = lax.dot_general(x_ref[...], w_ref[0, i], NN, preferred_element_type=F32).astype(BF16)
        pre_ref[0, i] = pre
        ext[...] = pre.astype(F32)
        total = conv_forward(ext, taps_ref[0, i], age, rows)
        act = total * sigmoid(total)
        if i < 2:
            act = act * l2_ratio(act)
        act = act.astype(BF16)
        qkv_ref[0, i] = act
        out.append(act)
    _, key, value = out
    beta = beta_ref[0]
    gram = lax.dot_general(key, key, NT, preferred_element_type=F32)
    lower = jnp.where(same & (col < row), beta * gram, 0.0)
    inverse = unit_lower_inverse(lower)
    tt_ref[0] = inverse.T
    scaled = beta * jnp.concatenate([key, value], -1).astype(F32)
    solved = mm(inverse, scaled)
    y_ref[0] = solved
    w_part, u_part = solved[:, :HD], solved[:, HD:]
    ms_ref[0, 0] = keep * (eye - mm(w_part, key, TN))
    ms_ref[0, 1] = mm(last * u_part, key, TN)


def output_kernel(*refs, sources):
    arrived, (y_ref, qkv_ref, lb_ref, gain_ref, o_ref, r_ref, s_ref, n_ref) = refs[:sources], refs[sources:]
    rows = lb_ref.shape[0]
    lb = lb_ref[...]
    row = lax.broadcasted_iota(jnp.int32, (rows, rows), 0)
    col = lax.broadcasted_iota(jnp.int32, (rows, rows), 1)
    carried = jnp.where(lb < 0, 1.0, 0.0)
    state = arrived[-1][0, 1]
    for ref in reversed(arrived[:-1]):
        state = mm(state, ref[0, 0]) + ref[0, 1]
    query, key = qkv_ref[0, 0], qkv_ref[0, 1]
    w_part, u_part = y_ref[0, :, :HD], y_ref[0, :, HD:]
    scores = lax.dot_general(query, key, NT, preferred_element_type=F32)
    scores = jnp.where((col >= lb) & (col <= row), scores * SCALE, 0.0)
    fresh = u_part - carried * mm(w_part, state, NT)
    mixed = carried * (SCALE * mm(query, state, NT)) + mm(scores, fresh)
    o_ref[0] = mixed
    r_ref[0] = fresh
    s_ref[0] = state
    ratio = lax.rsqrt(jnp.mean(mixed * mixed, -1, keepdims=True) + EPS)
    n_ref[...] = (mixed * ratio * gain_ref[...]).astype(BF16)


def mixed_back_kernel(g_ref, o_ref, qkv_ref, y_ref, lb_ref, lbr_ref, gain_ref, do_ref, dr_ref, ds_ref, hg_ref):
    rows = lb_ref.shape[0]
    row = lax.broadcasted_iota(jnp.int32, (rows, rows), 0)
    col = lax.broadcasted_iota(jnp.int32, (rows, rows), 1)
    carried = jnp.where(lb_ref[...] < 0, 1.0, 0.0)
    mixed, grad = o_ref[0], g_ref[...]
    ratio = lax.rsqrt(jnp.mean(mixed * mixed, -1, keepdims=True) + EPS)
    scaled = mixed * ratio
    weighted = grad * gain_ref[...]
    d_mixed = ratio * (weighted - scaled * jnp.mean(weighted * scaled, -1, keepdims=True))
    hg_ref[0] = jnp.broadcast_to(jnp.sum(grad * scaled, 0, keepdims=True), (8, HD))
    query, key = qkv_ref[0, 0], qkv_ref[0, 1]
    turned = lax.dot_general(key, query, NT, preferred_element_type=F32)
    turned = jnp.where((row >= lbr_ref[...]) & (row <= col), turned * SCALE, 0.0)
    d_fresh = mm(turned, d_mixed)
    do_ref[0] = d_mixed
    dr_ref[0] = d_fresh
    ds_ref[0] = SCALE * mm(carried * d_mixed, query, TN) - mm(carried * d_fresh, y_ref[0, :, :HD], TN)


def terms_back_kernel(*refs, sources):
    grads, maps = refs[:sources], refs[sources : 2 * sources - 1]
    (pre_ref, qkv_ref, tt_ref, y_ref, r_ref, s_ref, do_ref, dr_ref, beta_ref, taps_ref, lb_ref, lbr_ref,
     g_ref, gb_ref, cg_ref, ext, acc) = refs[2 * sources - 1 :]
    rows = lb_ref.shape[0]
    lb = lb_ref[...]
    place = lax.broadcasted_iota(jnp.int32, (rows, 1), 0)
    age = place - lb
    row = lax.broadcasted_iota(jnp.int32, (rows, rows), 0)
    col = lax.broadcasted_iota(jnp.int32, (rows, rows), 1)
    lb_last = lb_ref[pl.ds(rows - 1, 1), :]
    last = jnp.where(place >= lb_last, 1.0, 0.0)
    carried = jnp.where(lb < 0, 1.0, 0.0)
    same = col >= lb
    d_state = grads[-1][0]
    for grad, turn in zip(reversed(grads[:-1]), reversed(maps), strict=True):
        d_state = mm(d_state, turn[0, 0], NT) + grad[0]
    query, key, value = qkv_ref[0, 0], qkv_ref[0, 1], qkv_ref[0, 2]
    solved = y_ref[0]
    fresh, state, d_mixed = r_ref[0], s_ref[0], do_ref[0]
    beta = beta_ref[0]
    d_fresh = dr_ref[0] + last * mm(key, d_state, NT)
    lower_eq = same & (col <= row)
    d_scores = jnp.where(lower_eq, SCALE * mm(d_mixed, fresh, NT), 0.0)
    turned = jnp.where((row >= lbr_ref[...]) & (row <= col), SCALE * mm(fresh, d_mixed, NT), 0.0)
    d_query = mm(d_scores, key) + carried * (SCALE * mm(d_mixed, state))
    d_key = mm(turned, query) + mm(last * fresh, d_state)
    d_solved = jnp.concatenate([-carried * mm(d_fresh, state), d_fresh], -1)
    d_scaled = mm(tt_ref[0], d_solved)
    d_value = beta * d_scaled[:, HD:]
    d_key = d_key + beta * d_scaled[:, :HD]
    d_beta = jnp.sum(d_scaled[:, :HD] * key.astype(F32) + d_scaled[:, HD:] * value.astype(F32), -1, keepdims=True)
    gram = lax.dot_general(key, key, NT, preferred_element_type=F32)
    d_lower = jnp.where(same & (col < row), -mm(d_scaled, solved, NT), 0.0)
    d_beta = d_beta + jnp.sum(d_lower * gram, -1, keepdims=True)
    d_gram = beta * d_lower
    d_key = d_key + mm(d_gram, key) + mm(d_gram, key, TN)
    gb_ref[0] = d_beta * beta * (1.0 - beta)
    acc[...] = jnp.zeros_like(acc)
    for i, grad in enumerate((d_query, d_key, d_value)):
        taps = taps_ref[0, i]
        ext[...] = pre_ref[0, i].astype(F32)
        total = conv_forward(ext, taps, age, rows)
        sig = sigmoid(total)
        if i < 2:
            act = total * sig
            ratio = l2_ratio(act)
            unit = act * ratio
            grad = ratio * (grad - unit * jnp.sum(grad * unit, -1, keepdims=True))
        grad = grad * sig * (1.0 + total * (1.0 - sig))
        back = jnp.zeros((rows + PAD, HD), F32)
        for k in range(CONV):
            reach = CONV - 1 - k
            grad_k = jnp.where(age >= reach, grad, 0.0)
            rows_k = ext[pl.ds(PAD - reach, rows), :]
            cg_ref[0, pl.ds(i * CONV + k, 1), :] = jnp.sum(grad_k * rows_k, 0, keepdims=True)
            acc[pl.ds(PAD, rows), :] = grad_k
            back = back + acc[pl.ds(reach, rows + PAD), :] * taps[k : k + 1]
        g_ref[0, i] = back


def head_spec(*shape):
    return pl.BlockSpec((1,) + shape, lambda h: (h,) + (0,) * len(shape))


def whole_spec(*shape):
    return pl.BlockSpec(shape, lambda h: (0,) * len(shape))


def params():
    return pltpu.CompilerParams(vmem_limit_bytes=56 * 1024 * 1024, dimension_semantics=("arbitrary",))


def sds(*shape, dtype=F32):
    return jax.ShapeDtypeStruct(shape, dtype)


def delta_terms(x_ext, weights, taps, beta, lb):
    heads, rows = beta.shape[0], lb.shape[0]
    width = x_ext.shape[1]
    ext = rows + PAD
    return pl.pallas_call(
        terms_kernel,
        name="delta_terms",
        grid=(heads,),
        in_specs=[whole_spec(ext, width), head_spec(3, width, HD), head_spec(3, CONV, HD), head_spec(rows, 1), whole_spec(rows, 1)],
        out_specs=[head_spec(3, ext, HD), head_spec(3, rows, HD), head_spec(rows, rows), head_spec(rows, 2 * HD), head_spec(2, HD, HD)],
        out_shape=[
            sds(heads, 3, ext, HD, dtype=BF16),
            sds(heads, 3, rows, HD, dtype=BF16),
            sds(heads, rows, rows),
            sds(heads, rows, 2 * HD),
            sds(heads, 2, HD, HD),
        ],
        scratch_shapes=[pltpu.VMEM((ext, HD), F32)],
        compiler_params=params(),
        cost_estimate=pl.CostEstimate(flops=heads * 4_000_000_000, bytes_accessed=8_000_000, transcendentals=0),
    )(x_ext, weights, taps, beta, lb)


def delta_outputs(arrived, solved, qkv, lb, gain):
    heads, rows = solved.shape[0], lb.shape[0]
    return pl.pallas_call(
        functools.partial(output_kernel, sources=len(arrived)),
        name="delta_outputs",
        grid=(heads,),
        in_specs=[head_spec(2, HD, HD)] * len(arrived)
        + [head_spec(rows, 2 * HD), head_spec(3, rows, HD), whole_spec(rows, 1), whole_spec(1, HD)],
        out_specs=[head_spec(rows, HD), head_spec(rows, HD), head_spec(HD, HD), pl.BlockSpec((rows, HD), lambda h: (0, h))],
        out_shape=[sds(heads, rows, HD), sds(heads, rows, HD), sds(heads, HD, HD), sds(rows, heads * HD, dtype=BF16)],
        compiler_params=params(),
        cost_estimate=pl.CostEstimate(flops=heads * 1_000_000_000, bytes_accessed=5_000_000, transcendentals=0),
    )(*arrived, solved, qkv, lb, gain)


def mixed_back(head_grad, mixed, qkv, solved, lb, lb_row, gain):
    heads, rows = solved.shape[0], lb.shape[0]
    return pl.pallas_call(
        mixed_back_kernel,
        name="mixed_back",
        grid=(heads,),
        in_specs=[
            pl.BlockSpec((rows, HD), lambda h: (0, h)),
            head_spec(rows, HD),
            head_spec(3, rows, HD),
            head_spec(rows, 2 * HD),
            whole_spec(rows, 1),
            whole_spec(1, rows),
            whole_spec(1, HD),
        ],
        out_specs=[head_spec(rows, HD), head_spec(rows, HD), head_spec(HD, HD), head_spec(8, HD)],
        out_shape=[sds(heads, rows, HD), sds(heads, rows, HD), sds(heads, HD, HD), sds(heads, 8, HD)],
        compiler_params=params(),
        cost_estimate=pl.CostEstimate(flops=heads * 1_000_000_000, bytes_accessed=5_000_000, transcendentals=0),
    )(head_grad, mixed, qkv, solved, lb, lb_row, gain)


def terms_back(grads, maps, pre, qkv, turned, solved, fresh, state, d_mixed, d_fresh, beta, taps, lb, lb_row):
    heads, rows = solved.shape[0], lb.shape[0]
    ext = rows + PAD
    return pl.pallas_call(
        functools.partial(terms_back_kernel, sources=len(grads)),
        name="terms_back",
        grid=(heads,),
        in_specs=[head_spec(HD, HD)] * len(grads)
        + [head_spec(1, HD, HD)] * len(maps)
        + [
            head_spec(3, ext, HD),
            head_spec(3, rows, HD),
            head_spec(rows, rows),
            head_spec(rows, 2 * HD),
            head_spec(rows, HD),
            head_spec(HD, HD),
            head_spec(rows, HD),
            head_spec(rows, HD),
            head_spec(rows, 1),
            head_spec(3, CONV, HD),
            whole_spec(rows, 1),
            whole_spec(1, rows),
        ],
        out_specs=[head_spec(3, ext, HD), head_spec(rows, 1), head_spec(16, HD)],
        out_shape=[sds(heads, 3, ext, HD), sds(heads, rows, 1), sds(heads, 16, HD)],
        scratch_shapes=[pltpu.VMEM((ext, HD), F32), pltpu.VMEM((ext + PAD, HD), F32)],
        compiler_params=params(),
        cost_estimate=pl.CostEstimate(flops=heads * 3_000_000_000, bytes_accessed=8_000_000, transcendentals=0),
    )(*grads, *maps, pre, qkv, turned, solved, fresh, state, d_mixed, d_fresh, beta, taps, lb, lb_row)


def shifted(value, axis, steps):
    count = lax.axis_size(axis)
    first, end = max(0, -steps), min(count, count - steps)
    return lax.ppermute(value, axis, [(s, s + steps) for s in range(first, end)])


def swapped(value, axis, mask):
    return lax.ppermute(value, axis, [(s, s ^ mask) for s in range(lax.axis_size(axis))])


def tp_sum(value):
    return value + swapped(value, "tp", 1)


def plane_gather(value):
    half = value.shape[0] // 2
    one, two = swapped(value, "ctx", 1), swapped(value, "ctx", 2)
    three = jnp.concatenate([swapped(one[:half], "ctx", 2), swapped(two[half:], "ctx", 1)])
    return [value, one, two, three]


def in_order(pieces):
    here = lax.axis_index("ctx")
    stacked = jnp.stack(pieces)
    return [lax.dynamic_index_in_dim(stacked, here ^ k, 0, False) for k in range(len(pieces))]


def plane_reduce(own, first_one, first_two, second_one, second_two):
    from_one = [swapped(v.astype(BF16), "ctx", 1) for v in first_one]
    from_two = [swapped(v.astype(BF16), "ctx", 2) for v in first_two]
    late_two = swapped((second_two + from_one[1].astype(F32)).astype(BF16), "ctx", 2)
    late_one = swapped((second_one + from_two[1].astype(F32)).astype(BF16), "ctx", 1)
    half_a = own[0] + from_one[0].astype(F32) + late_two.astype(F32)
    half_b = own[1] + from_two[0].astype(F32) + late_one.astype(F32)
    return half_a.astype(BF16), half_b.astype(BF16)


def butterfly(value):
    for axis in ("ctx", "fsdp"):
        mask = 1
        while mask < lax.axis_size(axis):
            value = value + swapped(value, axis, mask)
            mask *= 2
    return value


def rms_norm(values, gain):
    return values * lax.rsqrt(jnp.mean(values * values, -1, keepdims=True) + EPS) * gain


def norm_back(values, gain, grad):
    ratio = lax.rsqrt(jnp.mean(values * values, -1, keepdims=True) + EPS)
    scaled = values * ratio
    weighted = grad * gain
    value_grad = ratio * (weighted - scaled * jnp.mean(weighted * scaled, -1, keepdims=True))
    return value_grad, jnp.sum(grad * scaled, 0)


def row_total(values, valid):
    return jnp.sum(valid * jnp.sum(values * values, -1))


def bdot(left, right, dims=NN):
    return lax.dot_general(left, right, dims, preferred_element_type=F32)


def local(
    tokens, lengths, norm_gain, qkv_weight, beta_weight, conv_weight, head_gain, out_weight, mlp_gain, gate_up_weight, down_weight, cotangent
):
    rows, width = tokens.shape
    n_ctx, n_fsdp = lax.axis_size("ctx"), lax.axis_size("fsdp")
    ctx, fsdp = lax.axis_index("ctx"), lax.axis_index("fsdp")
    d_loc = qkv_weight.shape[1]
    heads = beta_weight.shape[1]
    units = down_weight.shape[0]
    hk = heads * HD
    hd_loc = head_gain.shape[0]

    first = ctx * rows
    ends, total = [], 0
    for i in range(lengths.shape[1]):
        total = total + lengths[0, i]
        ends.append(total)
    place = first + lax.broadcasted_iota(jnp.int32, (rows, 1), 0)
    begins = jnp.zeros((rows, 1), jnp.int32)
    for end in ends:
        begins = jnp.where(end <= place, jnp.maximum(begins, end), begins)
    lb = begins - first
    lb_row = lb.reshape(1, rows)
    valid = (place < ends[-1]).astype(F32)
    valid_row = valid[:, 0]

    small = jnp.concatenate([norm_gain, mlp_gain, head_gain, beta_weight.reshape(-1), conv_weight.reshape(-1)])
    small_rows = -(-small.shape[0] // (HD * 16)) * 16
    small = jnp.pad(small, (0, small_rows * HD - small.shape[0])).reshape(small_rows, HD)
    qkv_part = lax.dynamic_slice_in_dim(qkv_weight, ctx * HD, HD, 2).reshape(3 * d_loc, HD)
    pack = lax.all_gather(jnp.concatenate([qkv_part, small]), "fsdp", axis=0)
    out_part = lax.dynamic_slice_in_dim(out_weight, ctx * HD, HD, 0)
    down_part = lax.dynamic_slice_in_dim(down_weight, ctx * (units // n_ctx), units // n_ctx, 0)
    od_all = lax.all_gather(jnp.concatenate([out_part, down_part]), "fsdp", axis=0)
    gu_rows = d_loc // n_ctx
    gu_part = lax.dynamic_slice_in_dim(gate_up_weight, ctx * gu_rows, gu_rows, 1)
    gu_all = lax.all_gather(gu_part, "fsdp", axis=0)

    qkv_heads = in_order(plane_gather(pack[:, : 3 * d_loc]))
    qkv_heads = jnp.stack([p.reshape(n_fsdp, 3, d_loc, HD).transpose(1, 0, 2, 3).reshape(3, width, HD) for p in qkv_heads])
    od = in_order(plane_gather(od_all))
    od = [p.transpose(1, 0, 2).reshape(-1, width) for p in od]
    out_full = jnp.concatenate([p[:HD] for p in od])
    down_full = jnp.concatenate([p[HD:] for p in od])
    gu = jnp.stack(in_order(plane_gather(gu_all)))
    gate_up_full = gu.transpose(2, 1, 0, 3, 4).reshape(2, width, units)

    flat = pack[:, 3 * d_loc :].reshape(n_fsdp, -1).astype(F32)
    at = 0
    first_gain = flat[:, at : at + d_loc].reshape(1, width)
    at += d_loc
    second_gain = flat[:, at : at + d_loc].reshape(1, width)
    at += d_loc
    head_full = flat[:, at : at + hd_loc].reshape(1, HD)
    at += hd_loc
    beta_full = flat[:, at : at + d_loc * heads].reshape(width, heads).astype(BF16)
    at += d_loc * heads
    conv_full = flat[:, at : at + 3 * CONV * heads * hd_loc].reshape(n_fsdp, 3, CONV, heads, hd_loc)
    conv_full = conv_full.transpose(3, 1, 2, 0, 4).reshape(heads, 3, CONV, HD)

    x_ext = jnp.concatenate([shifted(tokens[rows - PAD :], "ctx", 1), tokens])
    normed_ext = rms_norm(x_ext.astype(F32), first_gain).astype(BF16)
    normed_in = normed_ext[PAD:]
    x_wide = tokens.astype(F32)
    beta = jax.nn.sigmoid(bdot(normed_in, beta_full)).T.reshape(heads, rows, 1)
    pre, qkv, turned, solved, ends_map = delta_terms(normed_ext, qkv_heads, conv_full, beta, lb)

    arrived = [shifted(ends_map, "ctx", r) for r in range(1, n_ctx)]
    ahead = [shifted(ends_map[:, :1], "ctx", -r) for r in range(1, n_ctx - 1)]
    mixed, fresh, state, head_out = delta_outputs(arrived, solved, qkv, lb, head_full)

    attn = tp_sum(bdot(head_out, out_full)) * valid
    middle = x_wide + attn
    normed_mid = rms_norm(middle, second_gain).astype(BF16)
    gate = bdot(normed_mid, gate_up_full[0])
    up = bdot(normed_mid, gate_up_full[1])
    sig = jax.nn.sigmoid(gate)
    act = (gate * sig * up).astype(BF16)
    ffn = tp_sum(bdot(act, down_full)) * valid
    result = middle + ffn

    cot = cotangent.astype(F32)
    g_ffn = (cot * valid).astype(BF16)
    g_act = bdot(g_ffn, down_full, NT)
    g_up = (g_act * gate * sig).astype(BF16)
    g_gate = (g_act * up * sig * (1.0 + gate * (1.0 - sig))).astype(BF16)
    mid_part = bdot(g_gate, gate_up_full[0], NT) + bdot(g_up, gate_up_full[1], NT)

    def by_ctx(value, axis):
        return [lax.dynamic_index_in_dim(value, ctx ^ j, axis, False) for j in range(n_ctx)]

    act_t = act.T.reshape(n_ctx, 2, units // n_ctx // 2, rows)
    act_p = by_ctx(act_t, 0)
    down_g = [[bdot(p[h], g_ffn) for h in range(2)] for p in act_p]
    down_sum = plane_reduce(
        down_g[0], [down_g[1][0], down_g[3][0]], [down_g[2][1], down_g[3][1]], down_g[1][1], down_g[2][0]
    )
    down_sum = jnp.concatenate(down_sum).reshape(-1, n_fsdp, d_loc)
    down_sh = lax.psum_scatter(down_sum, "fsdp", scatter_dimension=1)

    g_gu = jnp.concatenate([g_gate, g_up], -1)
    mid_t = normed_mid.T.reshape(n_fsdp, n_ctx, 2, gu_rows // 2, rows).transpose(1, 2, 0, 3, 4)
    mid_p = by_ctx(mid_t, 0)
    gu_g = [[bdot(p[h].reshape(-1, rows), g_gu) for h in range(2)] for p in mid_p]
    gu_sum = plane_reduce(gu_g[0], [gu_g[1][0], gu_g[3][0]], [gu_g[2][1], gu_g[3][1]], gu_g[1][1], gu_g[2][0])
    gu_sum = jnp.stack(gu_sum).reshape(2, n_fsdp, gu_rows // 2, 2 * units)
    gu_sh = lax.psum_scatter(gu_sum, "fsdp", scatter_dimension=1)

    mid_grad = tp_sum(mid_part)
    mid_norm_grad, second_gain_grad = norm_back(middle, second_gain, mid_grad)
    g_middle = cot + mid_norm_grad
    g_attn = (g_middle * valid).astype(BF16)
    g_head = bdot(g_attn, out_full, NT)

    head_t = head_out.T.reshape(n_ctx, 2, HD // 2, rows)
    head_p = by_ctx(head_t, 0)
    out_g = [[bdot(p[h], g_attn) for h in range(2)] for p in head_p]
    out_sum = plane_reduce(out_g[0], [out_g[1][0], out_g[3][0]], [out_g[2][1], out_g[3][1]], out_g[1][1], out_g[2][0])
    out_sum = jnp.concatenate(out_sum).reshape(-1, n_fsdp, d_loc)
    out_sh = lax.psum_scatter(out_sum, "fsdp", scatter_dimension=1)

    d_mixed, d_fresh, d_state, head_gain_part = mixed_back(g_head, mixed, qkv, solved, lb, lb_row, head_full)
    behind = [shifted(d_state, "ctx", -r) for r in range(1, n_ctx)]
    g_ext, g_logit, conv_grad = terms_back(
        behind, ahead, pre, qkv, turned, solved, fresh, state, d_mixed, d_fresh, beta, conv_full, lb, lb_row
    )
    rim = shifted(g_ext[:, :, PAD - (CONV - 1) : PAD], "ctx", -1)
    g_pre = jnp.concatenate([g_ext[:, :, PAD : PAD + rows - (CONV - 1)], g_ext[:, :, PAD + rows - (CONV - 1) :] + rim], 2).astype(BF16)
    g_logit = g_logit[:, :, 0].astype(BF16)

    in_t = normed_in.T.reshape(n_fsdp, 2, d_loc // 2, rows).transpose(1, 0, 2, 3).reshape(2, width // 2, rows)
    g_p = [p.transpose(1, 0, 2).reshape(rows, 3 * HD) for p in by_ctx(g_pre, 0)]
    qkv_g = [[bdot(in_t[h], p) for h in range(2)] for p in g_p]
    qkv_sum = plane_reduce(qkv_g[0], [qkv_g[1][0], qkv_g[3][0]], [qkv_g[2][1], qkv_g[3][1]], qkv_g[1][1], qkv_g[2][0])
    qkv_sum = jnp.stack(qkv_sum).reshape(2, n_fsdp, d_loc // 2, 3 * HD)
    qkv_sh = lax.psum_scatter(qkv_sum, "fsdp", scatter_dimension=1)

    in_part = bdot(g_logit, beta_full, (((0,), (1,)), ((), ())))
    g_rows = g_pre.transpose(2, 1, 0, 3).reshape(rows, 3, hk)
    qkv_wide = qkv_heads.transpose(1, 2, 0, 3).reshape(3, width, hk)
    for i in range(3):
        in_part = in_part + bdot(g_rows[:, i], qkv_wide[i], NT)
    head_gain_row = jnp.pad(jnp.sum(head_gain_part[:, 0], 0), (0, width - HD))
    in_all = tp_sum(jnp.concatenate([in_part, jnp.broadcast_to(head_gain_row[None], (8, width))]))
    x_norm_grad, first_gain_grad = norm_back(x_wide, first_gain, in_all[:rows])
    input_grad = g_middle + x_norm_grad
    beta_grad = bdot(normed_in, g_logit, (((0,), (1,)), ((), ())))

    stats = jnp.stack([row_total(v, valid_row) for v in (x_wide, attn, middle, ffn, result)] + [jnp.sum(valid_row)])
    sums = butterfly(
        jnp.concatenate(
            [first_gain_grad, second_gain_grad, in_all[rows, :HD], beta_grad.reshape(-1), conv_grad[:, : 3 * CONV].reshape(-1), stats]
        )
    )
    at = 0
    first_out = lax.dynamic_slice_in_dim(sums[at : at + width], fsdp * d_loc, d_loc)
    at += width
    second_out = lax.dynamic_slice_in_dim(sums[at : at + width], fsdp * d_loc, d_loc)
    at += width
    head_out_grad = lax.dynamic_slice_in_dim(sums[at : at + HD], fsdp * hd_loc, hd_loc)
    at += HD
    beta_out = lax.dynamic_slice_in_dim(sums[at : at + width * heads].reshape(width, heads), fsdp * d_loc, d_loc)
    at += width * heads
    conv_out = sums[at : at + heads * 3 * CONV * HD].reshape(heads, 3, CONV, HD).transpose(1, 2, 0, 3)
    conv_out = lax.dynamic_slice_in_dim(conv_out, fsdp * hd_loc, hd_loc, 3)
    at += heads * 3 * CONV * HD
    stat = sums[at : at + 6]
    rms = jnp.sqrt(stat[:5] / (stat[5] * width))

    def whole(part):
        pieces = [part] + [swapped(part, "ctx", j) for j in range(1, n_ctx)]
        return jnp.stack(in_order(pieces)).astype(F32)

    down_out = whole(down_sh).reshape(units, d_loc)
    gu_out = whole(gu_sh).reshape(d_loc, 2, units).transpose(1, 0, 2)
    out_out = whole(out_sh).reshape(hk, d_loc)
    qkv_out = whole(qkv_sh).reshape(n_ctx, d_loc, 3, HD).transpose(2, 1, 0, 3).reshape(3, d_loc, hk)
    return (
        result.astype(BF16),
        input_grad,
        first_out,
        qkv_out,
        beta_out,
        conv_out,
        head_out_grad,
        out_out,
        second_out,
        gu_out,
        down_out,
        rms,
    )


def solution(mesh):
    return jax.shard_map(
        local,
        mesh=mesh,
        in_specs=(
            P(("fsdp", "ctx"), None),
            P("fsdp", None),
            P("fsdp"),
            P(None, "fsdp", "tp"),
            P("fsdp", "tp"),
            P(None, None, "tp", "fsdp"),
            P("fsdp"),
            P("tp", "fsdp"),
            P("fsdp"),
            P(None, "fsdp", "tp"),
            P("tp", "fsdp"),
            P(("fsdp", "ctx"), None),
        ),
        out_specs=(
            P(("fsdp", "ctx"), None),
            P(("fsdp", "ctx"), None),
            P("fsdp"),
            P(None, "fsdp", "tp"),
            P("fsdp", "tp"),
            P(None, None, "tp", "fsdp"),
            P("fsdp"),
            P("tp", "fsdp"),
            P("fsdp"),
            P(None, "fsdp", "tp"),
            P("tp", "fsdp"),
            P(),
        ),
        check_vma=False,
    )
```

time: 1160 us -> 530 us (0.46)
  waiting for transfers between devices: 684 us -> 130 us
  matrix products: 210 us -> 46.3 us
  starting transfers between devices: 24 us -> 87.2 us
  blocking collectives: 103 us -> 41.6 us
  Pallas kernels: 0 us -> 51.6 us
  other arithmetic: 28.9 us -> 52.1 us
    reduce_scatter x4, waiting for transfers between devices: 291 us -> 0.05 us  [the longest x1 0.02 us: local(): down_sh = lax.psum_scatter(down_sum, 'fsdp', scatter_dimension=1)]
    all_gather x4 -> x1, waiting for transfers between devices: 172 us -> 0.02 us  [local(): gu_all = lax.all_gather(gu_part, 'fsdp', axis=0)]
    dot_general x137 -> x46, matrix products: 209 us -> 46.3 us  [bdot(): return lax.dot_general(left, right, dims, preferred_element_type=F32)]
    psum x4 -> x0, waiting for transfers between devices: 145 us -> none  [the longest x1 103 us: local(): lax.psum((shares[0], shares[1], shares[2], shares[3], shares[4], shares[5...]
    ppermute x8 -> x66, waiting for transfers between devices: 34.1 us -> 130 us  [the longest x56 116 us: swapped(): lax.ppermute(value, axis, [(s, s ^ mask) for s in range(lax.axis_size(axi...]
    ppermute x8 -> x66, starting transfers between devices: 23.2 us -> 86.7 us  [the longest x56 66.5 us: swapped(): lax.ppermute(value, axis, [(s, s ^ mask) for s in range(lax.axis_size(axi...]
    pallas_call x0 -> x4, Pallas kernels: none -> 51.6 us  [the longest x1 26.3 us: delta_terms(): pl.pallas_call(terms_kernel, name='delta_terms', grid=(heads,), in_specs=...]
    unnamed x16 -> x5, waiting for transfers between devices: 40.8 us -> 0.08 us
  transfers between devices with their start and end apart: 22 -> 71, of which waited for: 18 -> 37; matrix products, arithmetic and copies ran while one was open for 25% -> 27% of each run, Pallas kernels for 0% -> 10%
where the time goes in v1:
time: 530 us; the launch traced here: 522 us
  waiting for transfers between devices  130 us (25%)
  local copies, waits for them, and re-layouts  93.4 us (18%)
  starting transfers between devices  87.2 us (16%)
  other arithmetic  52.1 us (10%)
  Pallas kernels  51.6 us (10%)
  matrix products  46.3 us (9%)
  blocking collectives  41.6 us (8%)
  between operations  19.8 us (4%)
    ppermute x56, waiting for transfers between devices, swapped(): lax.ppermute(value, axis, [(s, s ^ mask) for s in range(lax.axis_size(axi...  116 us
    ppermute x56, starting transfers between devices, swapped(): lax.ppermute(value, axis, [(s, s ^ mask) for s in range(lax.axis_size(axi...  66.5 us
    dot_general x46, matrix products, bdot(): return lax.dot_general(left, right, dims, preferred_element_type=F32)  46.3 us
    pallas_call x1, Pallas kernels, delta_terms(): pl.pallas_call(terms_kernel, name='delta_terms', grid=(heads,), in_specs=...  26.3 us
    all_gather x1, blocking collectives, local(): pack = lax.all_gather(jnp.concatenate([qkv_part, small]), 'fsdp', axis=0)  21.7 us
    ppermute x10, starting transfers between devices, shifted(): lax.ppermute(value, axis, [(s, s + steps) for s in range(first, end)])  20.2 us
    all_gather x1, blocking collectives, local(): lax.all_gather(jnp.concatenate([out_part, down_part]), 'fsdp', axis=0)  19.9 us
    unnamed x157, local copies, waits for them, and re-layouts  13.6 us
  transfers between devices with their start and end apart: 71, of which 37 were waited for; matrix products, arithmetic and copies ran while one was open for 27% of the time, Pallas kernels for 10%

profile of v1, /device:TPU:0, one launch (start us, length us, event | category | flops | bytes accessed | tf_op | source)
XLA Modules:
  0.0 521.6 jit_solution(16113444243930862200)
XLA Ops:
  12.2 21.7 %all-gather = bf16[3200,128]{1,0:T(8,128)(2,1)S(1)} all-gather(bf16[800,128]{1,0:T(8,128)(2,1)S(1)} %pad_maximum_fusion.23), channel_id=2, replica_groups=mesh['fsdp'=4,'ctx'=4,'tp'=2] {'fsdp'}, dimensions={0}, use_global_device_ids=true | all-gather | bytes 1024000 | tf_op jit(solution)/shard_map/all_gather | solution.py:421
  40.9 19.9 %all-gather.1 = bf16[1920,256]{1,0:T(8,128)(2,1)S(1)} all-gather(bf16[480,256]{1,0:T(8,128)(2,1)S(1)} %pad_maximum_fusion.22), channel_id=3, replica_groups=mesh['fsdp'=4,'ctx'=4,'tp'=2] {'fsdp'}, dimensions={0}, use_global_device_ids=true | all-gather | bytes 1228800 | tf_op jit(solution)/shard_map/all_gather | solution.py:424
  61.9 3.4 collective-permute-start
  74.4 5.8 %collective-permute-done = bf16[8,1024]{1,0:T(8,128)(2,1)S(1)} collective-permute-done((bf16[8,1024]{1,0:T(8,128)(2,1)S(1)}, bf16[8,1024]{1,0:T(8,128)(2,1)S(1)}, u32[]{:S(2)}, u32[]{:S(2)}) %collective-permute-start) | collective-permute-done | bytes 16416 | tf_op jit(solution)/shard_map/ppermute | solution.py:328
  94.3 2.9 collective-permute-done.3
  100.5 3.0 fusion.93
  103.5 26.3 %delta_terms.1 = (bf16[4,3,264,128]{3,2,1,0:T(8,128)(2,1)}, bf16[4,3,256,128]{3,2,1,0:T(8,128)(2,1)}, f32[4,256,256]{2,1,0:T(8,128)}, f32[4,256,256]{2,1,0:T(8,128)}, f32[4,2,128,128]{3,2,1,0:T(8,128)}) custom-call(bf16[264,1024]{1,0:T(8,128)(2,1)} %copy-done.8, bf16[4,3,1024,128]{3,2,1,0:T(8,128)(2,1)} %get-tuple-element.115.w_ref, ...), custom_call_target="tpu_custom_call" | custom-call | flops 16000000000 | bytes 8000000 | tf_op jit(solution)/shard_map/delta_terms/pallas_call | solution.py:238
  129.8 3.7 collective-permute-start.5
  149.6 6.5 %delta_outputs.1 = (f32[4,256,128]{2,1,0:T(8,128)}, f32[4,256,128]{2,1,0:T(8,128)}, f32[4,128,128]{2,1,0:T(8,128)}, bf16[256,512]{1,0:T(8,128)(2,1)}) custom-call(f32[4,2,128,128]{3,2,1,0:T(8,128)} %collective-permute-done.5.refs_0_, f32[4,2,128,128]{3,2,1,0:T(8,128)} %collective-permute-done.6.refs_1_, f32[4,2,128,128]{3,2,1,0:T(8,128)} %collective-permute-done.7.refs_2_, ...), custom_call_target="tpu_custom_call" | custom-call | flops 4000000000 | bytes 5000000 | tf_op jit(solution)/shard_map/delta_outputs/pallas_call | solution.py:259
  164.2 3.6 fusion.96
  185.9 7.1 %collective-permute-done.14 = bf16[4,2,64,1408]{3,2,1,0:T(8,128)(2,1)} collective-permute-done((bf16[4,2,64,1408]{3,2,1,0:T(8,128)(2,1)}, bf16[4,2,64,1408]{3,2,1,0:T(8,128)(2,1)}, u32[]{:S(2)}, u32[]{:S(2)}) %collective-permute-start.14) | collective-permute-done | bytes 1441824 | tf_op jit(solution)/shard_map/ppermute | solution.py:332
  199.6 13.3 %collective-permute-done.16 = bf16[2,2,64,1408]{3,2,1,0:T(8,128)(2,1)} collective-permute-done((bf16[2,2,64,1408]{3,2,1,0:T(8,128)(2,1)}, bf16[2,2,64,1408]{3,2,1,0:T(8,128)(2,1)}, u32[]{:S(2)}, u32[]{:S(2)}) %collective-permute-start.16) | collective-permute-done | bytes 720928 | tf_op jit(solution)/shard_map/ppermute | solution.py:332
  216.5 3.4 pad_maximum_fusion
  256.0 16.2 %collective-permute-done.61 = bf16[176,1024]{1,0:T(8,128)(2,1)S(1)} collective-permute-done((bf16[176,1024]{1,0:T(8,128)(2,1)S(1)}, bf16[176,1024]{1,0:T(8,128)(2,1)S(1)}, u32[]{:S(2)}, u32[]{:S(2)}) %collective-permute-start.61) | collective-permute-done | bytes 360480 | tf_op jit(solution)/shard_map/ppermute | solution.py:332
  281.3 10.0 %collective-permute-done.49 = bf16[128,2816]{1,0:T(8,128)(2,1)S(1)} collective-permute-done((bf16[128,2816]{1,0:T(8,128)(2,1)S(1)}, bf16[128,2816]{1,0:T(8,128)(2,1)S(1)}, u32[]{:S(2)}, u32[]{:S(2)}) %collective-permute-start.49) | collective-permute-done | bytes 720928 | tf_op jit(solution)/shard_map/ppermute | solution.py:332
  303.8 3.7 collective-permute-done.40
  310.3 3.2 collective-permute-done.44
  331.9 5.4 %mixed_back.1 = (f32[4,256,128]{2,1,0:T(8,128)}, f32[4,256,128]{2,1,0:T(8,128)}, f32[4,128,128]{2,1,0:T(8,128)}, f32[4,8,128]{2,1,0:T(8,128)}) custom-call(f32[256,512]{1,0:T(8,128)} %fusion.41.g_ref, f32[4,256,128]{2,1,0:T(8,128)} %get-tuple-element.32.o_ref, bf16[4,3,256,128]{3,2,1,0:T(8,128)(2,1)} %get-tuple-element.30.refs_4_.qkv_ref.refs_6_, ...), custom_call_target="tpu_custom_call" | custom-call | flops 4000000000 | bytes 5000000 | tf_op jit(solution)/shard_map/mixed_back/pallas_call | solution.py:274
  343.3 3.7 collective-permute-start.51
  348.9 4.2 collective-permute-done.20.refs_1_
  356.3 13.3 %terms_back.1 = (f32[4,3,264,128]{3,2,1,0:T(8,128)}, f32[4,256,1]{2,1,0:T(8,128)}, f32[4,16,128]{2,1,0:T(8,128)}) custom-call(f32[4,128,128]{2,1,0:T(8,128)} %copy-done.71, f32[4,128,128]{2,1,0:T(8,128)} %copy-done.72, f32[4,128,128]{2,1,0:T(8,128)} %copy-done.73, f32[4,1,128,128]{3,2,1,0:T(8,128)} %collective-permute-done.22.refs_3_, ...), custom_call_target="tpu_custom_call" | custom-call | flops 12000000000 | bytes 8000000 | tf_op jit(solution)/shard_map/terms_back/pallas_call | solution.py:297
  400.5 3.5 collective-permute-done.31
  408.1 8.8 %collective-permute-done.35 = bf16[512,384]{1,0:T(8,128)(2,1)S(1)} collective-permute-done((bf16[512,384]{1,0:T(8,128)(2,1)S(1)}, bf16[512,384]{1,0:T(8,128)(2,1)S(1)}, u32[]{:S(2)}, u32[]{:S(2)}) %collective-permute-start.35) | collective-permute-done | bytes 393248 | tf_op jit(solution)/shard_map/ppermute | solution.py:332
  420.6 2.9 add_convert_fusion
  423.5 4.9 collective-permute-done.48
  428.5 3.1 collective-permute-done.50
  453.9 3.8 concatenate.60
  466.1 7.3 %collective-permute-done.28 = f32[12422]{0:T(1024)S(1)} collective-permute-done((f32[12422]{0:T(1024)S(1)}, f32[12422]{0:T(1024)S(1)}, u32[]{:S(2)}, u32[]{:S(2)}) %collective-permute-start.28) | collective-permute-done | bytes 49720 | tf_op jit(solution)/shard_map/ppermute | solution.py:332
  475.1 4.4 collective-permute-done.29
  500.6 3.3 collective-permute-done.55
  506.1 4.7 reshape.407
  510.8 3.7 copy.155
  (492 shorter events, 271.2 us)
Async XLA Ops:
  7.2 151.5 %all-gather.5.cloned.1.call-start = ((), (), s32[]{:S(2)}) async-start(), calls=%async_computation.8 | async-start | bytes 1802240 | tf_op jit(solution)/shard_map/all_gather | solution.py:427
  36.0 44.4 %collective-permute-start.2 = (bf16[4,768,128]{2,1,0:T(8,128)(2,1)}, bf16[4,768,128]{2,1,0:T(8,128)(2,1)}, u32[]{:S(2)}, u32[]{:S(2)}) collective-permute-start(bf16[4,768,128]{2,1,0:T(8,128)(2,1)} %get-tuple-element.129), channel_id=1, source_target_pairs={{0,4},{2,6},{4,0},{6,2},{1,5},{3,7},{5,1},{7,3},{8,12},{10,14},{12... | collective-permute-start | bytes 2359304 | tf_op jit(solution)/shard_map/ppermute | solution.py:332
  37.6 46.7 %collective-permute-start.1 = (bf16[4,768,128]{2,1,0:T(8,128)(2,1)}, bf16[4,768,128]{2,1,0:T(8,128)(2,1)}, u32[]{:S(2)}, u32[]{:S(2)}) collective-permute-start(bf16[4,768,128]{2,1,0:T(8,128)(2,1)} %get-tuple-element.129), channel_id=1, source_target_pairs={{0,2},{2,0},{4,6},{6,4},{1,3},{3,1},{5,7},{7,5},{8,10},{10,8},{12,... | collective-permute-start | bytes 2359304 | tf_op jit(solution)/shard_map/ppermute | solution.py:332
  60.8 28.7 %collective-permute-start.9 = (bf16[4,480,256]{2,1,0:T(8,128)(2,1)S(1)}, bf16[4,480,256]{2,1,0:T(8,128)(2,1)}, u32[]{:S(2)}, u32[]{:S(2)}) collective-permute-start(bf16[4,480,256]{2,1,0:T(8,128)(2,1)S(1)} %bitcast.371), channel_id=1, source_target_pairs={{0,4},{2,6},{4,0},{6,2},{1,5},{3,7},{5,1},{7,3},{8,12},{10,14},{12... | collective-permute-start | bytes 2949128 | tf_op jit(solution)/shard_map/ppermute | solution.py:332
  61.3 31.3 %collective-permute-start.8 = (bf16[4,480,256]{2,1,0:T(8,128)(2,1)S(1)}, bf16[4,480,256]{2,1,0:T(8,128)(2,1)}, u32[]{:S(2)}, u32[]{:S(2)}) collective-permute-start(bf16[4,480,256]{2,1,0:T(8,128)(2,1)S(1)} %bitcast.372), channel_id=1, source_target_pairs={{0,2},{2,0},{4,6},{6,4},{1,3},{3,1},{5,7},{7,5},{8,10},{10,8},{12,... | collective-permute-start | bytes 2949128 | tf_op jit(solution)/shard_map/ppermute | solution.py:332
  61.9 18.4 %collective-permute-start = (bf16[8,1024]{1,0:T(8,128)(2,1)S(1)}, bf16[8,1024]{1,0:T(8,128)(2,1)S(1)}, u32[]{:S(2)}, u32[]{:S(2)}) collective-permute-start(bf16[8,1024]{1,0:T(8,128)(2,1)S(1)} %slice.296), channel_id=1, source_target_pairs={{0,2},{2,4},{4,6},{1,3},{3,5},{5,7},{8,10},{10,12},{12,14},{9,11},... | collective-permute-start | bytes 49160 | tf_op jit(solution)/shard_map/ppermute | solution.py:328
  66.1 367.9 %reduce-scatter.7.cloned.1.call-start = ((), (), s32[]{:S(2)}) async-start(), calls=%async_computation.5 | async-start | bytes 327680 | tf_op jit(solution)/shard_map/reduce_scatter | solution.py:510
  90.6 47.9 %collective-permute-start.11 = (bf16[2,480,256]{2,1,0:T(8,128)(2,1)S(1)}, bf16[2,480,256]{2,1,0:T(8,128)(2,1)S(1)}, u32[]{:S(2)}, u32[]{:S(2)}) collective-permute-start(bf16[2,480,256]{2,1,0:T(8,128)(2,1)S(1)} %slice.390), channel_id=1, source_target_pairs={{0,2},{2,0},{4,6},{6,4},{1,3},{3,1},{5,7},{7,5},{8,10},{10,8},{12,... | collective-permute-start | bytes 1474568 | tf_op jit(solution)/shard_map/ppermute | solution.py:332
  93.7 44.8 %collective-permute-start.10 = (bf16[2,480,256]{2,1,0:T(8,128)(2,1)S(1)}, bf16[2,480,256]{2,1,0:T(8,128)(2,1)S(1)}, u32[]{:S(2)}, u32[]{:S(2)}) collective-permute-start(bf16[2,480,256]{2,1,0:T(8,128)(2,1)S(1)} %slice.389), channel_id=1, source_target_pairs={{0,4},{2,6},{4,0},{6,2},{1,5},{3,7},{5,1},{7,3},{8,12},{10,14},{12... | collective-permute-start | bytes 1474568 | tf_op jit(solution)/shard_map/ppermute | solution.py:332
  129.8 19.8 %collective-permute-start.5 = (f32[4,2,128,128]{3,2,1,0:T(8,128)}, f32[4,2,128,128]{3,2,1,0:T(8,128)}, u32[]{:S(2)}, u32[]{:S(2)}) collective-permute-start(f32[4,2,128,128]{3,2,1,0:T(8,128)} %get-tuple-element.28), channel_id=1, source_target_pairs={{0,2},{2,4},{4,6},{1,3},{3,5},{5,7},{8,10},{10,12},{12,14},{9,11},... | collective-permute-start | bytes 1572872 | tf_op jit(solution)/shard_map/ppermute | solution.py:328
  158.6 25.2 %collective-permute-start.12 = (f32[256,1024]{1,0:T(8,128)}, f32[256,1024]{1,0:T(8,128)}, u32[]{:S(2)}, u32[]{:S(2)}) collective-permute-start(f32[256,1024]{1,0:T(8,128)} %fusion.42), channel_id=1, source_target_pairs={{0,1},{1,0},{2,3},{3,2},{4,5},{5,4},{6,7},{7,6},{8,9},{9,8},{10,11... | collective-permute-start | bytes 3145736 | tf_op jit(solution)/shard_map/ppermute | solution.py:332
  158.7 34.3 %collective-permute-start.14 = (bf16[4,2,64,1408]{3,2,1,0:T(8,128)(2,1)}, bf16[4,2,64,1408]{3,2,1,0:T(8,128)(2,1)}, u32[]{:S(2)}, u32[]{:S(2)}) collective-permute-start(bf16[4,2,64,1408]{3,2,1,0:T(8,128)(2,1)} %bitcast.415), channel_id=1, source_target_pairs={{0,4},{2,6},{4,0},{6,2},{1,5},{3,7},{5,1},{7,3},{8,12},{10,14},{12... | collective-permute-start | bytes 4325384 | tf_op jit(solution)/shard_map/ppermute | solution.py:332
  158.7 36.2 %collective-permute-start.13 = (bf16[4,2,64,1408]{3,2,1,0:T(8,128)(2,1)}, bf16[4,2,64,1408]{3,2,1,0:T(8,128)(2,1)}, u32[]{:S(2)}, u32[]{:S(2)}) collective-permute-start(bf16[4,2,64,1408]{3,2,1,0:T(8,128)(2,1)} %bitcast.416), channel_id=1, source_target_pairs={{0,2},{2,0},{4,6},{6,4},{1,3},{3,1},{5,7},{7,5},{8,10},{10,8},{12,... | collective-permute-start | bytes 4325384 | tf_op jit(solution)/shard_map/ppermute | solution.py:332
  195.0 18.0 %collective-permute-start.16 = (bf16[2,2,64,1408]{3,2,1,0:T(8,128)(2,1)}, bf16[2,2,64,1408]{3,2,1,0:T(8,128)(2,1)}, u32[]{:S(2)}, u32[]{:S(2)}) collective-permute-start(bf16[2,2,64,1408]{3,2,1,0:T(8,128)(2,1)} %slice.397), channel_id=1, source_target_pairs={{0,2},{2,0},{4,6},{6,4},{1,3},{3,1},{5,7},{7,5},{8,10},{10,8},{12,... | collective-permute-start | bytes 2162696 | tf_op jit(solution)/shard_map/ppermute | solution.py:332
  197.0 18.0 %collective-permute-start.15 = (bf16[2,2,64,1408]{3,2,1,0:T(8,128)(2,1)}, bf16[2,2,64,1408]{3,2,1,0:T(8,128)(2,1)}, u32[]{:S(2)}, u32[]{:S(2)}) collective-permute-start(bf16[2,2,64,1408]{3,2,1,0:T(8,128)(2,1)} %slice.396), channel_id=1, source_target_pairs={{0,4},{2,6},{4,0},{6,2},{1,5},{3,7},{5,1},{7,3},{8,12},{10,14},{12... | collective-permute-start | bytes 2162696 | tf_op jit(solution)/shard_map/ppermute | solution.py:332
  245.3 47.2 %collective-permute-start.18 = (f32[256,1024]{1,0:T(8,128)S(1)}, f32[256,1024]{1,0:T(8,128)S(1)}, u32[]{:S(2)}, u32[]{:S(2)}) collective-permute-start(f32[256,1024]{1,0:T(8,128)S(1)} %convolution_add_fusion.1), channel_id=1, source_target_pairs={{0,1},{1,0},{2,3},{3,2},{4,5},{5,4},{6,7},{7,6},{8,9},{9,8},{10,11... | collective-permute-start | bytes 3145736 | tf_op jit(solution)/shard_map/ppermute | solution.py:332
  245.5 47.0 %collective-permute-start.17 = (f32[256,1024]{1,0:T(8,128)S(1)}, f32[256,1024]{1,0:T(8,128)S(1)}, u32[]{:S(2)}, u32[]{:S(2)}) collective-permute-start(f32[256,1024]{1,0:T(8,128)S(1)} %copy-done.43), channel_id=1, source_target_pairs={{0,1},{1,0},{2,3},{3,2},{4,5},{5,4},{6,7},{7,6},{8,9},{9,8},{10,11... | collective-permute-start | bytes 3145736 | tf_op jit(solution)/shard_map/ppermute | solution.py:332
  246.2 31.4 %collective-permute-start.52 = (bf16[128,2816]{1,0:T(8,128)(2,1)S(1)}, bf16[128,2816]{1,0:T(8,128)(2,1)S(1)}, u32[]{:S(2)}, u32[]{:S(2)}) collective-permute-start(bf16[128,2816]{1,0:T(8,128)(2,1)S(1)} %convolution_convert_fusion), channel_id=1, source_target_pairs={{0,4},{2,6},{4,0},{6,2},{1,5},{3,7},{5,1},{7,3},{8,12},{10,14},{12... | collective-permute-start | bytes 2162696 | tf_op jit(solution)/shard_map/ppermute | solution.py:332
  251.1 21.1 %collective-permute-start.61 = (bf16[176,1024]{1,0:T(8,128)(2,1)S(1)}, bf16[176,1024]{1,0:T(8,128)(2,1)S(1)}, u32[]{:S(2)}, u32[]{:S(2)}) collective-permute-start(bf16[176,1024]{1,0:T(8,128)(2,1)S(1)} %convolution_convert_fusion.8), channel_id=1, source_target_pairs={{0,4},{2,6},{4,0},{6,2},{1,5},{3,7},{5,1},{7,3},{8,12},{10,14},{12... | collective-permute-start | bytes 1081352 | tf_op jit(solution)/shard_map/ppermute | solution.py:332
  253.0 22.1 %collective-permute-start.58 = (bf16[176,1024]{1,0:T(8,128)(2,1)S(1)}, bf16[176,1024]{1,0:T(8,128)(2,1)S(1)}, u32[]{:S(2)}, u32[]{:S(2)}) collective-permute-start(bf16[176,1024]{1,0:T(8,128)(2,1)S(1)} %convolution_convert_fusion.10), channel_id=1, source_target_pairs={{0,2},{2,0},{4,6},{6,4},{1,3},{3,1},{5,7},{7,5},{8,10},{10,8},{12,... | collective-permute-start | bytes 1081352 | tf_op jit(solution)/shard_map/ppermute | solution.py:332
  272.2 19.1 %collective-permute-start.49 = (bf16[128,2816]{1,0:T(8,128)(2,1)S(1)}, bf16[128,2816]{1,0:T(8,128)(2,1)S(1)}, u32[]{:S(2)}, u32[]{:S(2)}) collective-permute-start(bf16[128,2816]{1,0:T(8,128)(2,1)S(1)} %convolution_convert_fusion.2), channel_id=1, source_target_pairs={{0,2},{2,0},{4,6},{6,4},{1,3},{3,1},{5,7},{7,5},{8,10},{10,8},{12,... | collective-permute-start | bytes 2162696 | tf_op jit(solution)/shard_map/ppermute | solution.py:332
  275.0 68.3 %collective-permute-start.22 = (f32[4,1,128,128]{3,2,1,0:T(8,128)}, f32[4,1,128,128]{3,2,1,0:T(8,128)}, u32[]{:S(2)}, u32[]{:S(2)}) collective-permute-start(f32[4,1,128,128]{3,2,1,0:T(8,128)} %slice.333), channel_id=1, source_target_pairs={{2,0},{4,2},{6,4},{3,1},{5,3},{7,5},{10,8},{12,10},{14,12},{11,9},... | collective-permute-start | bytes 786440 | tf_op jit(solution)/shard_map/ppermute | solution.py:328
  277.6 45.5 %collective-permute-start.60 = (bf16[176,1024]{1,0:T(8,128)(2,1)}, bf16[176,1024]{1,0:T(8,128)(2,1)}, u32[]{:S(2)}, u32[]{:S(2)}) collective-permute-start(bf16[176,1024]{1,0:T(8,128)(2,1)} %convolution_convert_fusion.9), channel_id=1, source_target_pairs={{0,4},{2,6},{4,0},{6,2},{1,5},{3,7},{5,1},{7,3},{8,12},{10,14},{12... | collective-permute-start | bytes 1081352 | tf_op jit(solution)/shard_map/ppermute | solution.py:332
  291.3 33.1 %collective-permute-start.62 = (bf16[176,1024]{1,0:T(8,128)(2,1)}, bf16[176,1024]{1,0:T(8,128)(2,1)}, u32[]{:S(2)}, u32[]{:S(2)}) collective-permute-start(bf16[176,1024]{1,0:T(8,128)(2,1)} %add_convert_fusion.9), channel_id=1, source_target_pairs={{0,2},{2,0},{4,6},{6,4},{1,3},{3,1},{5,7},{7,5},{8,10},{10,8},{12,... | collective-permute-start | bytes 1081352 | tf_op jit(solution)/shard_map/ppermute | solution.py:332
  323.0 118.0 %reduce-scatter.11.cloned.1.call-start = ((), (), s32[]{:S(2)}) async-start(), calls=%async_computation.7 | async-start | bytes 901120 | tf_op jit(solution)/shard_map/reduce_scatter | solution.py:489
  323.1 23.9 %collective-permute-start.23 = (f32[4,1,128,128]{3,2,1,0:T(8,128)}, f32[4,1,128,128]{3,2,1,0:T(8,128)}, u32[]{:S(2)}, u32[]{:S(2)}) collective-permute-start(f32[4,1,128,128]{3,2,1,0:T(8,128)} %slice.333), channel_id=1, source_target_pairs={{4,0},{6,2},{5,1},{7,3},{12,8},{14,10},{13,9},{15,11},{20,16},{22,... | collective-permute-start | bytes 786440 | tf_op jit(solution)/shard_map/ppermute | solution.py:328
  330.3 154.4 %reduce-scatter.5.cloned.1.call-start = ((), (), s32[]{:S(2)}) async-start(), calls=%async_computation.4 | async-start | bytes 983040 | tf_op jit(solution)/shard_map/reduce_scatter | solution.py:526
  343.3 77.3 %collective-permute-start.51 = (bf16[128,2816]{1,0:T(8,128)(2,1)}, bf16[128,2816]{1,0:T(8,128)(2,1)}, u32[]{:S(2)}, u32[]{:S(2)}) collective-permute-start(bf16[128,2816]{1,0:T(8,128)(2,1)} %convolution_convert_fusion.1), channel_id=1, source_target_pairs={{0,4},{2,6},{4,0},{6,2},{1,5},{3,7},{5,1},{7,3},{8,12},{10,14},{12... | collective-permute-start | bytes 2162696 | tf_op jit(solution)/shard_map/ppermute | solution.py:332
  347.0 73.7 %collective-permute-start.53 = (bf16[128,2816]{1,0:T(8,128)(2,1)}, bf16[128,2816]{1,0:T(8,128)(2,1)}, u32[]{:S(2)}, u32[]{:S(2)}) collective-permute-start(bf16[128,2816]{1,0:T(8,128)(2,1)} %add_convert_fusion.1), channel_id=1, source_target_pairs={{0,2},{2,0},{4,6},{6,4},{1,3},{3,1},{5,7},{7,5},{8,10},{10,8},{12,... | collective-permute-start | bytes 2162696 | tf_op jit(solution)/shard_map/ppermute | solution.py:332
  398.8 20.1 %collective-permute-start.30 = (bf16[512,384]{1,0:T(8,128)(2,1)S(1)}, bf16[512,384]{1,0:T(8,128)(2,1)S(1)}, u32[]{:S(2)}, u32[]{:S(2)}) collective-permute-start(bf16[512,384]{1,0:T(8,128)(2,1)S(1)} %convolution_convert_fusion.7), channel_id=1, source_target_pairs={{0,2},{2,0},{4,6},{6,4},{1,3},{3,1},{5,7},{7,5},{8,10},{10,8},{12,... | collective-permute-start | bytes 1179656 | tf_op jit(solution)/shard_map/ppermute | solution.py:332
  419.0 32.8 %collective-permute-start.25 = (f32[264,1024]{1,0:T(8,128)}, f32[264,1024]{1,0:T(8,128)}, u32[]{:S(2)}, u32[]{:S(2)}) collective-permute-start(f32[264,1024]{1,0:T(8,128)} %pad_maximum_fusion.9), channel_id=1, source_target_pairs={{0,1},{1,0},{2,3},{3,2},{4,5},{5,4},{6,7},{7,6},{8,9},{9,8},{10,11... | collective-permute-start | bytes 3244040 | tf_op jit(solution)/shard_map/ppermute | solution.py:332
  420.3 68.4 %reduce-scatter.9.cloned.1.call-start = ((), (), s32[]{:S(2)}) async-start(), calls=%async_computation.6 | async-start | bytes 1802240 | tf_op jit(solution)/shard_map/reduce_scatter | solution.py:497
  (113 other events, 802.8 us)
Sparse Core Ops, SparseCore 0:
  66.2 33.4 all-gather.4
  323.2 18.5 reduce-scatter.6
  344.2 21.1 reduce-scatter.10
  420.4 22.7 reduce-scatter.4
  446.0 34.7 reduce-scatter.8
